TPU v7x, 512 devices: a whole 4x4x16 slice. The times are simulated.
512 devices in a mesh: comp: 8 (over x, core), panel: 64 (over z, y).
Axes of the slice: x: 4, y: 4, z: 16, core: 2. Of those that a mesh axis runs over, the one named last changes fastest.
Arguments:
- state: float32 [8, 5, 64, 192, 256], P('comp', None, 'panel'), as said below
- time_step: float32 [8, 64, 192, 256], P('comp', 'panel'), may hold values from 10 to 40
- radius: float32 [8, 64, 192, 256], P('comp', 'panel'), may hold values from 0.5 to 4
- implicit_coeff: float32 [8, 3], P('comp'), may hold values from 9 to 36
- donor_cells: int32 [8, 64, 8, 512], P('comp', 'panel'), may hold values from 0 to 49151
- donor_weights: float32 [8, 64, 8, 512], P('comp', 'panel'), as said below
- donor_group: int32 [8, 64, 512, 1], P('comp', 'panel'), may hold values from 0 to 7; in each aligned block of 512 rows (0 to 511, 512 to 1023, ..., all dimensions but the last counted through in order) at most 128 rows name the same one
- recv_cells: int32 [8, 64, 8, 128], P('comp', 'panel'), may hold values from 0 to 49151, as said below
Outputs:
- delta: float32 [8, 5, 64, 192, 256], P('comp', None, 'panel')
Inputs may be any that keep to these rules, and one draw needn't show every extreme that they name: `donor_weights`: the eight weights of a donor are positive and sum to one. `donor_group`: on one device no grid receives more than 128 donors, and some grid receives exactly 128 from some devices. `recv_cells`: the slab indices of one device are all distinct. `state`: density is positive.
All inputs are finite; a program needn't handle non-finite values.
Results may differ from a plain program's by a relative error of at most 0.0003.
Values sent between devices are 32-bit elements; how exact they have to be, the bound alone decides.
A program may use at most 128 MiB of HBM per device.

v0:
```python
import jax
import jax.numpy as jnp
from jax import lax
from jax.sharding import PartitionSpec as P

GAS_FACTOR = 0.4
EXPLICIT_FOURTH = 0.0625
IMPLICIT_SECOND = 1.0
IMPLICIT_FOURTH = 0.125


def passed_along(value, axis, by):
    length = lax.axis_size(axis)
    pairs = [(i, i + by) for i in range(length) if 0 <= i + by < length]
    return lax.ppermute(value, axis, pairs)


def direction_flux(field, direction, density):
    speed = field[direction] / density
    pressure = GAS_FACTOR * (
        field[4] - 0.5 * (field[1] * field[1] + field[2] * field[2] + field[3] * field[3]) / density
    )
    rows_out = [field[direction]]
    for member in (1, 2, 3):
        if member == direction:
            rows_out.append(field[member] * speed + pressure)
        else:
            rows_out.append(field[member] * speed)
    rows_out.append((field[4] + pressure) * speed)
    return jnp.stack(rows_out)


def central(values, axis):
    length = values.shape[axis]
    widths = [(0, 0)] * values.ndim
    widths[axis] = (1, 1)
    padded = jnp.pad(values, widths)
    return 0.5 * (
        lax.slice_in_dim(padded, 2, length + 2, axis=axis)
        - lax.slice_in_dim(padded, 0, length, axis=axis)
    )


def fourth(values, axis):
    length = values.shape[axis]
    widths = [(0, 0)] * values.ndim
    widths[axis] = (2, 2)
    padded = jnp.pad(values, widths)
    parts = [
        lax.slice_in_dim(padded, shift_by, shift_by + length, axis=axis) for shift_by in range(5)
    ]
    return parts[0] - 4.0 * parts[1] + 6.0 * parts[2] - 4.0 * parts[3] + parts[4]


def line_inverse(length, coeff):
    index = jnp.arange(length)
    gap = jnp.abs(index[:, None] - index[None, :])
    matrix = jnp.where(
        gap == 0,
        1.0 + coeff * (2.0 * IMPLICIT_SECOND + 6.0 * IMPLICIT_FOURTH),
        jnp.where(
            gap == 1,
            -coeff * (IMPLICIT_SECOND + 4.0 * IMPLICIT_FOURTH),
            jnp.where(gap == 2, coeff * IMPLICIT_FOURTH, 0.0 * coeff),
        ),
    )
    factor = jnp.linalg.cholesky(matrix)
    identity = jnp.eye(length, dtype=matrix.dtype)
    lower_part = lax.linalg.triangular_solve(factor, identity, left_side=True, lower=True)
    return lax.linalg.triangular_solve(
        factor, lower_part, left_side=True, lower=True, transpose_a=True
    )


def apply_along_i(values, inverse):
    return jnp.einsum("ab,vkjb->vkja", inverse, values, precision=lax.Precision.HIGHEST)


def apply_along_j(values, inverse):
    return jnp.einsum("ab,vkbi->vkai", inverse, values, precision=lax.Precision.HIGHEST)


def apply_along_k(values, inverse):
    return jnp.einsum("ab,vbji->vaji", inverse, values, precision=lax.Precision.HIGHEST)


def interpolate(grid_slab, cells, weights):
    return jnp.sum(grid_slab[:, cells] * weights[None], axis=1)


def pack_slots(donor_values, group_col, count, capacity):
    onehot = (group_col[:, None] == jnp.arange(count, dtype=jnp.int32)[None, :]).astype(jnp.int32)
    ranks = jnp.sum((jnp.cumsum(onehot, axis=0) - 1) * onehot, axis=1)
    target = group_col * capacity + ranks
    buffer = jnp.zeros((5, count * capacity), jnp.float32).at[:, target].set(donor_values)
    live = jnp.zeros((count * capacity,), jnp.float32).at[target].set(1.0)
    return (buffer.reshape(5, count, capacity).transpose(1, 0, 2), live.reshape(count, 1, capacity))


def place_fringe(grid_slab, got_values, got_live, targets):
    flat_values = got_values.transpose(1, 0, 2).reshape(5, -1)
    flat_live = got_live.reshape(-1)
    flat_cells = targets.reshape(-1)
    current = grid_slab[:, flat_cells]
    return grid_slab.at[:, flat_cells].set(
        jnp.where(flat_live[None, :] > 0.5, flat_values, current)
    )


def k_neighbor(values, offset):
    return passed_along(values, "panel", offset)


def masked_flux(values, present):
    safe_density = jnp.where(present, values[0], 1.0)
    return direction_flux(values, 3, safe_density) * present.astype(jnp.float32)


def body(
    state, time_step, radius, implicit_coeff, donor_cells, donor_weights, donor_group, recv_cells
):
    field = state[0]
    layers = field.shape[1]
    rows_j = field.shape[2]
    cols_i = field.shape[3]
    grid_slab = field.reshape(5, -1)
    donor_values = interpolate(grid_slab, donor_cells[0, 0], donor_weights[0, 0])
    group_col = donor_group[0, 0, :, 0]
    count = lax.axis_size("comp")
    capacity = recv_cells.shape[3]
    buffer, live = pack_slots(donor_values, group_col, count, capacity)
    got_values, got_live = (
        lax.all_to_all(buffer, "comp", split_axis=0, concat_axis=0, tiled=True),
        lax.all_to_all(live, "comp", split_axis=0, concat_axis=0, tiled=True),
    )
    fringed = place_fringe(grid_slab, got_values, got_live, recv_cells[0, 0]).reshape(field.shape)
    density = fringed[0]
    convect_ij = central(direction_flux(fringed, 1, density), 3) + central(
        direction_flux(fringed, 2, density), 2
    )
    smooth_ij = fourth(fringed, 3) + fourth(fringed, 2)
    steps_local = time_step[0]
    spread = radius[0]
    panels = lax.axis_size("panel")
    inverse_i = line_inverse(cols_i, implicit_coeff[0, 0])
    inverse_j = line_inverse(rows_j, implicit_coeff[0, 1])
    inverse_k = line_inverse(layers * panels, implicit_coeff[0, 2])
    far_low = k_neighbor(fringed, 2)
    near_low = k_neighbor(fringed, 1)
    near_high = k_neighbor(fringed, -1)
    far_high = k_neighbor(fringed, -2)
    place = lax.axis_index("panel")
    low_present = place >= 1
    high_present = place <= panels - 2
    convect_k = 0.5 * (masked_flux(near_high, high_present) - masked_flux(near_low, low_present))
    smooth_k = far_low - 4.0 * near_low + 6.0 * fringed - 4.0 * near_high + far_high
    rhs = steps_local * (
        -(convect_ij + convect_k) - EXPLICIT_FOURTH * spread * (smooth_ij + smooth_k)
    )
    solved = apply_along_i(apply_along_j(rhs, inverse_j), inverse_i)
    moved = apply_along_k(
        lax.all_to_all(solved, "panel", split_axis=2, concat_axis=1, tiled=True), inverse_k
    )
    delta = lax.all_to_all(moved, "panel", split_axis=1, concat_axis=2, tiled=True)
    return delta[None]


def solution(mesh):
    placed = (
        P("comp", None, "panel", None, None),
        P("comp", "panel", None, None),
        P("comp", "panel", None, None),
        P("comp", None),
        P("comp", "panel", None, None),
        P("comp", "panel", None, None),
        P("comp", "panel", None, None),
        P("comp", "panel", None, None),
    )
    return jax.shard_map(
        body,
        mesh=mesh,
        in_specs=placed,
        out_specs=P("comp", None, "panel", None, None),
        check_vma=False,
    )
```

profile of v0, /device:TPU:24, one launch (start us, length us, event | category | flops | bytes accessed | tf_op | source)
XLA Modules:
  0.0 529.5 jit_solution(14355209904241548969)
XLA Ops:
  0.0 0.7 fusion.107
  0.8 1.1 reduce-window.6
  2.1 0.8 fusion.106
  2.9 0.7 compare_select_fusion.2
  3.6 3.0 scatter_custom_fusion
  6.6 4.3 all-to-all-start
  10.9 1.4 fusion.120
  15.2 11.7 %cholesky.115 = f32[128,128]{1,0:T(8,128)S(1)} custom-call(f32[128,128]{1,0:T(8,128)S(1)} %cholesky.284), custom_call_target="Cholesky" | custom-call | tf_op jit(solution)/shard_map/jit(cholesky)/cholesky | solution.py:67
  29.7 11.7 %cholesky.248 = f32[128,128]{1,0:T(8,128)S(1)} custom-call(f32[128,128]{1,0:T(8,128)S(1)} %cholesky.287), custom_call_target="Cholesky" | custom-call | tf_op jit(solution)/shard_map/jit(cholesky)/cholesky | solution.py:67
  41.5 13.5 %copy.69 = f32[1,5,1,192,256]{1,4,3,2,0:T(8,128)} copy(f32[1,5,1,192,256]{4,3,2,1,0:T(8,128)} %param.8) | data formatting | bytes 1966080 | tf_op args[0]
  55.0 0.7 multiply_bitcast_fusion
  55.7 9.8 %custom-call.40 = f32[1,128,128]{1,2,0:T(8,128)S(1)} custom-call(f32[1,128,128]{2,1,0:T(8,128)S(1)} %get-tuple-element.70), custom_call_target="InvertDiagBlocksLowerTriangular" | custom-call | tf_op jit(solution)/shard_map/jit(cholesky)/cholesky | solution.py:67
  65.9 5.8 %cholesky.233 = f32[64,64]{1,0:T(8,128)S(1)} custom-call(f32[64,64]{1,0:T(8,128)S(1)} %convolution_subtract_fusion.5), custom_call_target="Cholesky" | custom-call | tf_op jit(solution)/shard_map/jit(cholesky)/cholesky | solution.py:67
  71.8 0.6 compare_reduce_fusion.4
  72.4 0.7 compare_reduce_fusion.3
  74.6 19.9 %custom-call.41 = f32[2,128,128]{1,2,0:T(8,128)S(1)} custom-call(f32[2,128,128]{2,1,0:T(8,128)S(1)} %pad_maximum_fusion), custom_call_target="InvertDiagBlocksLowerTriangular" | custom-call | tf_op jit(solution)/shard_map/triangular_solve | solution.py:70
  94.5 0.3 fusion.76
  94.8 0.3 convolution_subtract_fusion.4
  95.6 0.3 convolution_subtract_fusion.2
  95.9 0.9 fusion.84
  96.8 9.8 %custom-call.42 = f32[1,128,128]{1,2,0:T(8,128)S(1)} custom-call(f32[1,128,128]{2,1,0:T(8,128)S(1)} %get-tuple-element.68), custom_call_target="InvertDiagBlocksLowerTriangular" | custom-call | tf_op jit(solution)/shard_map/jit(cholesky)/cholesky | solution.py:67
  107.1 11.7 %cholesky.261 = f32[128,128]{1,0:T(8,128)S(1)} custom-call(f32[128,128]{1,0:T(8,128)S(1)} %convolution_subtract_fusion.3), custom_call_target="Cholesky" | custom-call | tf_op jit(solution)/shard_map/jit(cholesky)/cholesky | solution.py:67
  118.9 0.7 compare_reduce_fusion.1
  120.9 4.0 while.3
  120.9 0.6 fusion.139
  121.5 1.4 bitcast_dynamic-update-slice_fusion.2
  122.9 0.6 fusion.139
  123.5 1.4 bitcast_dynamic-update-slice_fusion.2
  124.9 19.7 %custom-call.43 = f32[2,128,128]{1,2,0:T(8,128)S(1)} custom-call(f32[2,128,128]{2,1,0:T(8,128)S(1)} %get-tuple-element.20), custom_call_target="InvertDiagBlocksLowerTriangular" | custom-call | tf_op jit(solution)/shard_map/triangular_solve | solution.py:70
  145.1 0.3 fusion.87
  145.7 0.3 convolution_subtract_fusion
  146.3 18.9 %gather_fusion = f32[4096,5]{1,0:T(8,128)S(1)} fusion(f32[5,49152]{0,1:T(8,128)} %bitcast.150, s32[4096]{0:T(1024)S(1)} %broadcast_clamp_fusion), kind=kCustom, calls=%fused_computation | custom fusion | bytes 180224 | tf_op jit(solution)/shard_map/gather | solution.py:88
  165.2 0.7 multiply_reduce_fusion
  166.1 2.3 scatter_custom_fusion.1
  168.4 0.8 copy.71
  169.2 4.8 all-to-all-start.1
  174.0 5.4 %all-to-all-done.1 = f32[8,5,128]{2,1,0:T(8,128)S(1)} async-done(((f32[8,5,128]{2,1,0:T(8,128)}), f32[8,5,128]{2,1,0:T(8,128)S(1)}, u32[]{:S(2)}, u32[]{:S(2)}) %all-to-all-start.1) | async-done | bytes 20512 | tf_op jit(solution)/shard_map/all_to_all | solution.py:133
  179.6 25.8 %scatter_custom_fusion.2 = f32[5,49152]{0,1:T(8,128)} fusion(f32[5,49152]{0,1:T(8,128)} %bitcast.151, s32[1024]{0:T(1024)S(1)} %bitcast.164, f32[5,1024]{0,1:T(8,128)S(1)} %bitcast.155, pred[1024]{0:T(1024)(128)(4,1)S(1)} %compare_bitcast_fusion, s32[1024]{0:T(1024)S(1)} %broadcast_clamp_fusion.1), kind=kCustom, calls=%fused_computation.71 | custom fusion | flops 5120 | bytes 2495488 | tf_op jit(solution)/shard_map/scatter | solution.py:105
  205.5 69.6 %slice_reduce_fusion = (f32[49152]{0:T(1024)S(1)}, f32[49152]{0:T(1024)S(1)}, f32[49152]{0:T(1024)S(1)}, f32[49152]{0:T(1024)S(1)}, f32[49152]{0:T(1024)S(1)}) fusion(f32[5,49152]{0,1:T(8,128)} %scatter_custom_fusion.2), kind=kLoop, calls=%fused_computation.7 | loop fusion | bytes 1966080 | tf_op jit(solution)/shard_map/slice | solution.py:21
  275.1 14.8 %copy.73 = f32[5,1,192,256]{3,2,1,0:T(8,128)} copy(f32[5,1,192,256]{0,3,2,1:T(8,128)} %bitcast.152) | data formatting | bytes 1966080 | tf_op jit(solution)/shard_map/reshape | solution.py:136
  289.8 3.2 collective-permute-start.3
  293.0 6.0 %collective-permute-start = (f32[5,1,192,256]{3,2,1,0:T(8,128)}, f32[5,1,192,256]{3,2,1,0:T(8,128)S(1)}, u32[]{:S(2)}, u32[]{:S(2)}) collective-permute-start(f32[5,1,192,256]{3,2,1,0:T(8,128)} %copy.73), channel_id=1, source_target_pairs={{1,0},{2,1},{3,2},{4,3},{5,4},{6,5},{7,6},{8,7},{9,8},{10,9},{11,1... | collective-permute-start | bytes 2949128 | tf_op jit(solution)/shard_map/ppermute | solution.py:15
  299.0 2.4 collective-permute-start.2
  301.4 3.4 collective-permute-start.1
  304.8 0.7 constant_dynamic-update-slice_fusion
  305.7 0.8 add_dynamic-update-slice_fusion.3
  306.5 0.7 multiply_dynamic-update-slice_fusion.11
  307.3 0.7 multiply_dynamic-update-slice_fusion.10
  308.0 0.7 multiply_dynamic-update-slice_fusion.9
  308.7 47.3 %collective-permute-done.1 = f32[5,1,192,256]{3,2,1,0:T(8,128)S(1)} collective-permute-done((f32[5,1,192,256]{3,2,1,0:T(8,128)}, f32[5,1,192,256]{3,2,1,0:T(8,128)S(1)}, u32[]{:S(2)}, u32[]{:S(2)}) %collective-permute-start.1) | collective-permute-done | bytes 983072 | tf_op jit(solution)/shard_map/ppermute | solution.py:15
  356.6 3.5 collective-permute-done.2
  360.1 9.4 %convolution_bitcast_fusion.2 = f32[5,192,256]{2,1,0:T(8,128)S(1)} fusion(f32[5,1,192,256]{3,2,1,0:T(8,128)S(1)} %get-tuple-element.59, f32[5,1,192,256]{3,2,1,0:T(8,128)} %get-tuple-element.58, f32[5,1,192,256]{3,2,1,0:T(8,128)} %copy.73, f32[5,1,192,256]{3,2,1,0:T(8,128)} %collective-permute-done.3, f32[5,1,192,256]{3,2,1,0:T(8,128)S(1)} %collective-permute-done, ...), kind=kOutput, calls=%fused_computation.21 | convolution fusion | flops 574377984 | bytes 10371080 | tf_op jit(solution)/shard_map/ab,vkbi->vkai/dot_general | solution.py:80
  369.6 1.0 convolution_bitcast_fusion.1
  370.6 2.0 copy.82
  372.5 30.9 %all-to-all-start.2 = ((f32[5,1,192,256]{3,1,0,2:T(1,128)}), f32[5,1,192,256]{3,1,0,2:T(1,128)S(1)}, u32[]{:S(2)}, u32[]{:S(2)}) async-start(f32[5,1,192,256]{3,1,0,2:T(1,128)} %copy.82), calls=%async_computation.2 | async-start | bytes 1966080 | tf_op jit(solution)/shard_map/all_to_all | solution.py:162
  406.0 5.8 %cholesky.276 = f32[64,64]{1,0:T(8,128)S(1)} custom-call(f32[64,64]{1,0:T(8,128)S(1)} %add_multiply_fusion.2), custom_call_target="Cholesky" | custom-call | tf_op jit(solution)/shard_map/jit(cholesky)/cholesky | solution.py:67
  411.9 0.7 compare_reduce_fusion
  412.6 0.7 fusion.90
  413.3 4.9 custom-call.44
  418.6 36.3 %all-to-all-done.2 = f32[5,1,192,256]{3,1,0,2:T(1,128)S(1)} async-done(((f32[5,1,192,256]{3,1,0,2:T(1,128)}), f32[5,1,192,256]{3,1,0,2:T(1,128)S(1)}, u32[]{:S(2)}, u32[]{:S(2)}) %all-to-all-start.2) | async-done | bytes 983072 | tf_op jit(solution)/shard_map/all_to_all | solution.py:162
  455.1 1.3 convolution_bitcast_fusion
  456.4 0.7 copy.85
  457.1 70.6 %all_to_all.31 = f32[5,64,3,256]{3,2,0,1:T(4,128)S(1)} all-to-all(f32[5,64,3,256]{3,2,0,1:T(4,128)S(1)} %copy.85), channel_id=1, replica_groups=mesh['comp'=8,'panel'=64] {'panel'}, dimensions={1} | all-to-all | bytes 1966080 | tf_op jit(solution)/shard_map/all_to_all | solution.py:164
  527.9 1.4 broadcast_in_dim.106
  (79 shorter events, 5.3 us)
Async XLA Ops:
  0.0 55.0 %copy-start.3 = (s32[1,1,8,128]{3,2,1,0:T(8,128)S(1)}, s32[1,1,8,128]{3,2,1,0:T(8,128)}, u32[]{:S(2)}) copy-start(s32[1,1,8,128]{3,2,1,0:T(8,128)} %param.15) | copy-start | bytes 12292
  0.0 55.0 %copy-start.2 = (s32[1,1,8,512]{3,2,1,0:T(8,128)S(1)}, s32[1,1,8,512]{3,2,1,0:T(8,128)}, u32[]{:S(2)}) copy-start(s32[1,1,8,512]{3,2,1,0:T(8,128)} %param.12) | copy-start | bytes 49156
  0.0 55.0 %copy-start = (f32[1,1,192,256]{3,2,1,0:T(8,128)S(1)}, f32[1,1,192,256]{3,2,1,0:T(8,128)}, u32[]{:S(2)}) copy-start(f32[1,1,192,256]{3,2,1,0:T(8,128)} %param.10) | copy-start | bytes 589828
  0.0 165.2 %copy-start.1 = (f32[1,1,8,512]{3,2,1,0:T(8,128)S(1)}, f32[1,1,8,512]{3,2,1,0:T(8,128)}, u32[]{:S(2)}) copy-start(f32[1,1,8,512]{3,2,1,0:T(8,128)} %param.13) | copy-start | bytes 49156
  6.6 162.6 %all-to-all-start = ((f32[8,1,128]{2,1,0:T(1,128)}), f32[8,1,128]{2,1,0:T(1,128)S(1)}, u32[]{:S(2)}, u32[]{:S(2)}) async-start(f32[8,1,128]{2,1,0:T(1,128)} %bitcast.11), calls=%async_computation | async-start | bytes 8192 | tf_op jit(solution)/shard_map/all_to_all | solution.py:134
  169.2 10.2 %all-to-all-start.1 = ((f32[8,5,128]{2,1,0:T(8,128)}), f32[8,5,128]{2,1,0:T(8,128)S(1)}, u32[]{:S(2)}, u32[]{:S(2)}) async-start(f32[8,5,128]{2,1,0:T(8,128)} %bitcast.18), calls=%async_computation.1 | async-start | bytes 65536 | tf_op jit(solution)/shard_map/all_to_all | solution.py:133
  289.8 66.8 %collective-permute-start.3 = (f32[5,1,192,256]{3,2,1,0:T(8,128)}, f32[5,1,192,256]{3,2,1,0:T(8,128)}, u32[]{:S(2)}, u32[]{:S(2)}) collective-permute-start(f32[5,1,192,256]{3,2,1,0:T(8,128)} %copy.73), channel_id=1, source_target_pairs={{2,0},{3,1},{4,2},{5,3},{6,4},{7,5},{8,6},{9,7},{10,8},{11,9},{12,... | collective-permute-start | bytes 2949128 | tf_op jit(solution)/shard_map/ppermute | solution.py:15
  293.0 63.1 %collective-permute-start = (f32[5,1,192,256]{3,2,1,0:T(8,128)}, f32[5,1,192,256]{3,2,1,0:T(8,128)S(1)}, u32[]{:S(2)}, u32[]{:S(2)}) collective-permute-start(f32[5,1,192,256]{3,2,1,0:T(8,128)} %copy.73), channel_id=1, source_target_pairs={{1,0},{2,1},{3,2},{4,3},{5,4},{6,5},{7,6},{8,7},{9,8},{10,9},{11,1... | collective-permute-start | bytes 2949128 | tf_op jit(solution)/shard_map/ppermute | solution.py:15
  299.0 61.1 %collective-permute-start.2 = (f32[5,1,192,256]{3,2,1,0:T(8,128)}, f32[5,1,192,256]{3,2,1,0:T(8,128)}, u32[]{:S(2)}, u32[]{:S(2)}) collective-permute-start(f32[5,1,192,256]{3,2,1,0:T(8,128)} %copy.73), channel_id=1, source_target_pairs={{0,2},{1,3},{2,4},{3,5},{4,6},{5,7},{6,8},{7,9},{8,10},{9,11},{10,... | collective-permute-start | bytes 2949128 | tf_op jit(solution)/shard_map/ppermute | solution.py:15
  301.4 54.7 %collective-permute-start.1 = (f32[5,1,192,256]{3,2,1,0:T(8,128)}, f32[5,1,192,256]{3,2,1,0:T(8,128)S(1)}, u32[]{:S(2)}, u32[]{:S(2)}) collective-permute-start(f32[5,1,192,256]{3,2,1,0:T(8,128)} %copy.73), channel_id=1, source_target_pairs={{0,1},{1,2},{2,3},{3,4},{4,5},{5,6},{6,7},{7,8},{8,9},{9,10},{10,1... | collective-permute-start | bytes 2949128 | tf_op jit(solution)/shard_map/ppermute | solution.py:15
  372.5 82.4 %all-to-all-start.2 = ((f32[5,1,192,256]{3,1,0,2:T(1,128)}), f32[5,1,192,256]{3,1,0,2:T(1,128)S(1)}, u32[]{:S(2)}, u32[]{:S(2)}) async-start(f32[5,1,192,256]{3,1,0,2:T(1,128)} %copy.82), calls=%async_computation.2 | async-start | bytes 1966080 | tf_op jit(solution)/shard_map/all_to_all | solution.py:162
where the time goes:
time: 538 us; the launch traced here: 530 us
  other arithmetic  149 us (28%)
  local copies, waits for them, and re-layouts  134 us (25%)
  waiting for transfers between devices  92.6 us (17%)
  blocking collectives  70.6 us (13%)
  starting transfers between devices  54.9 us (10%)
  matrix products  16.9 us (3%)
  between operations  11.2 us (2%)
    all_to_all x1, blocking collectives, body(): lax.all_to_all(moved, 'panel', split_axis=1, concat_axis=2, tiled=True)  70.6 us
    slice x1, local copies, waits for them, and re-layouts, direction_flux(): field[3] * field[3]  69.6 us
    another operation x16, other arithmetic, line_inverse(): factor = jnp.linalg.cholesky(matrix)  69.3 us
    ppermute x4, waiting for transfers between devices, passed_along(): return lax.ppermute(value, axis, pairs)  50.9 us
    another operation x11, other arithmetic, line_inverse(): lax.linalg.triangular_solve(factor, lower_part, left_side=True, lower=Tru...  45.3 us
    all_to_all x1, waiting for transfers between devices, body(): lax.all_to_all(solved, 'panel', split_axis=2, concat_axis=1, tiled=True)  36.3 us
    all_to_all x1, starting transfers between devices, body(): lax.all_to_all(solved, 'panel', split_axis=2, concat_axis=1, tiled=True)  30.9 us
    scatter x1, other arithmetic, place_fringe(): grid_slab.at[:, flat_cells]  25.8 us
  transfers between devices with their start and end apart: 7, of which 4 were waited for; matrix products, arithmetic and copies ran while one was open for 32% of the time, Pallas kernels for 0%

commit v1 on v0

v1 whole, which is shorter than its diff:
```python
import functools

import jax
import jax.numpy as jnp
from jax import lax
from jax.experimental import pallas as pl
from jax.experimental.pallas import tpu as pltpu
from jax.sharding import PartitionSpec as P

MESH = pl.DeviceIdType.MESH
F32, BF16 = jnp.float32, jnp.bfloat16
NV = 5
NY = 4
PAD = 8
ROWS = 16


def parts(x):
    hi = x.astype(BF16)
    rest = x - hi.astype(F32)
    mid = rest.astype(BF16)
    return hi, mid, (rest - mid.astype(F32)).astype(BF16)


def inverse_entries(h, length, i, j):
    root = jnp.sqrt(16.0 - 8.0 / h)
    m1, m2 = (8.0 / h) / (4.0 + root), 4.0 + root
    n = float(length)

    def green(m, a, b):
        s = 0.5 * jnp.sqrt(m)
        t = 2.0 * jnp.log(s + jnp.sqrt(1.0 + s * s))
        d = jnp.abs(a - b)
        top = (
            jnp.exp(-t * d)
            - jnp.exp(-t * (a + b + 2.0))
            - jnp.exp(-t * (2.0 * n - a - b))
            + jnp.exp(-t * (2.0 * n + 2.0 - d))
        )
        two_sinh = jnp.exp(t) - jnp.exp(-t)
        return top / (two_sinh * (1.0 - jnp.exp(-2.0 * t * (n + 1.0))))

    def smooth(a, b):
        return (8.0 / h) * (green(m1, a, b) - green(m2, a, b)) / (m2 - m1)

    zero = jnp.zeros_like(h)
    corner, across = smooth(zero, zero), smooth(zero, zero + (n - 1.0))
    even_scale = 0.5 / (8.0 / h + corner + across)
    odd_scale = 0.5 / (8.0 / h + corner - across)
    i0, i1 = smooth(i, zero), smooth(i, zero + (n - 1.0))
    j0, j1 = smooth(j, zero), smooth(j, zero + (n - 1.0))
    return (
        smooth(i, j)
        - even_scale * (i0 + i1) * (j0 + j1)
        - odd_scale * (i0 - i1) * (j0 - j1)
    )


def iota(shape, axis):
    return lax.broadcasted_iota(jnp.int32, shape, axis)


def donor_kernel(state, cells, weights, group, packed, left, acc):
    nv, nj, ni = state.shape
    n_c, don = cells.shape
    count = packed.shape[1] // 128
    width = min(256, don)
    flat = state[...].reshape(nv * nj, ni)
    for k, part in enumerate(parts(flat)):
        left[:, k * ni : (k + 1) * ni] = part
    acc[...] = jnp.zeros_like(acc)

    for block in range(don // width):
        span = slice(block * width, (block + 1) * width)

        def one(c, carry):
            cell = cells[pl.ds(c, 1), span]
            weight = weights[pl.ds(c, 1), span]
            col = jnp.where(iota((ni, width), 0) == cell % ni, 1.0, 0.0).astype(BF16)
            got = jnp.dot(
                left[...], jnp.concatenate([col, col, col], axis=0), preferred_element_type=F32
            )
            row = jnp.where(iota((nj, width), 0) == cell // ni, weight, 0.0)
            for v in range(nv):
                term = got[v * nj : (v + 1) * nj] * row
                acc[v, :, span] += jnp.sum(term.reshape(nj // 8, 8, width), axis=0)
            return carry

        lax.fori_loop(0, n_c, one, 0)

    values = [jnp.sum(acc[v], axis=0, keepdims=True) for v in range(nv)]
    values = jnp.concatenate(
        values + [jnp.ones((1, don), F32), jnp.zeros((8 - nv - 1, don), F32)], axis=0
    )
    mine = group[...]
    hot = jnp.where(iota((don, 128), 1) == mine, 1.0, 0.0)
    before = jnp.where(iota((don, don), 1) < iota((don, don), 0), 1.0, 0.0).astype(BF16)
    ahead = jnp.dot(before, hot.astype(BF16), preferred_element_type=F32)
    slot = jnp.sum(hot * ahead, axis=1, keepdims=True).astype(jnp.int32)
    target = mine * 128 + slot
    place = jnp.where(iota((don, count * 128), 1) == target, 1.0, 0.0).astype(BF16)
    hi, mid, lo = parts(values)
    packed[...] = (
        jnp.dot(hi, place, preferred_element_type=F32)
        + jnp.dot(mid, place, preferred_element_type=F32)
        + jnp.dot(lo, place, preferred_element_type=F32)
    )


def flux(f, direction):
    rho = jnp.where(f[0] > 0.0, f[0], 1.0)
    inv = 1.0 / rho
    speed = f[direction] * inv
    pressure = 0.4 * (f[4] - 0.5 * (f[1] * f[1] + f[2] * f[2] + f[3] * f[3]) * inv)
    out = [f[direction]]
    for member in (1, 2, 3):
        term = f[member] * speed
        out.append(term + pressure if member == direction else term)
    out.append((f[4] + pressure) * speed)
    return out


def step_kernel(
    nc, nz, state, step_size, radius, coeff, packed, cells, out,
    got, vals, full, slab, local, own, lin, lout, rin, rout, done, back, inv_j, inv_i, lhs, coef,
    fx_send, fx_recv, tr_send, tr_recv, ya_send, ya_recv, zh_send, zh_recv, sc_send, sc_recv, yb_send, yb_recv,
):
    _, nj, ni = state.shape
    quarter = nj // NY
    tall = quarter + 2 * PAD
    blocks = quarter // ROWS
    chunks = blocks * NV
    slots = vals.shape[1]
    me = lax.axis_index("comp")
    panel = lax.axis_index("panel")
    z, y = panel // NY, panel % NY
    low, high = (z + nz - 1) % nz, (z + 1) % nz

    def at(comp, z_, y_):
        return (comp, z_ * NY + y_)

    barrier = pltpu.get_barrier_semaphore()
    for d in range(1, nc):
        pl.semaphore_signal(barrier, inc=1, device_id=at((me + d) % nc, z, y), device_id_type=MESH)
    for d in range(1, NY):
        pl.semaphore_signal(barrier, inc=1, device_id=at(me, z, (y + d) % NY), device_id_type=MESH)
    pl.semaphore_signal(barrier, inc=1, device_id=at(me, low, y), device_id_type=MESH)
    pl.semaphore_signal(barrier, inc=1, device_id=at(me, high, y), device_id_type=MESH)
    pl.semaphore_wait(barrier, nc - 1 + NY - 1 + 2)

    def fringe(d):
        peer = (me + d) % nc
        return pltpu.make_async_remote_copy(
            src_ref=packed.at[:, pl.ds(pl.multiple_of(peer * 128, 128), 128)],
            dst_ref=got.at[me],
            send_sem=fx_send.at[d],
            recv_sem=fx_recv.at[d],
            device_id=at(peer, z, y),
            device_id_type=MESH,
        )

    for d in range(1, nc):
        fringe(d).start()

    def local_copy(which, d):
        to = (y + d) % NY
        return pltpu.make_async_remote_copy(
            src_ref=(step_size, radius)[which].at[pl.ds(pl.multiple_of(to * quarter, 8), quarter), :],
            dst_ref=local.at[which, y],
            send_sem=tr_send.at[which, d],
            recv_sem=tr_recv.at[which, d],
            device_id=at(me, z, to),
            device_id_type=MESH,
        )

    for which in range(2):
        for d in range(1, NY):
            local_copy(which, d).start()
    mine = pl.ds(pl.multiple_of(y * quarter, 8), quarter)
    local[0, y] = step_size[mine, :]
    local[1, y] = radius[mine, :]

    h2 = jnp.full((8, 128), coeff[0, 2], F32)
    base = (z * NY - 2).astype(F32)
    k_near = inverse_entries(
        h2,
        nz * NY,
        jnp.maximum(iota((8, 128), 0).astype(F32) + base, 0.0),
        jnp.maximum(iota((8, 128), 1).astype(F32) + base, 0.0),
    )

    def entry(a, b):
        return k_near[a : a + 1, b : b + 1]

    for q in range(4):
        for l in range(4):
            coef[q * 4 + l] = entry(2 + q, 2 + l)[0, 0]
    for side, first in ((0, 0), (1, 6)):
        a, b, d = entry(first, first), entry(first, first + 1), entry(first + 1, first + 1)
        det = 1.0 / (a * d - b * b)
        edge = (z == 0) if side == 0 else (z == nz - 1)
        for q in range(4):
            s, t = entry(2 + q, first), entry(2 + q, first + 1)
            coef[16 + side * 8 + q * 2] = jnp.where(edge, 0.0, ((s * d - t * b) * det)[0, 0])
            coef[16 + side * 8 + q * 2 + 1] = jnp.where(edge, 0.0, ((t * a - s * b) * det)[0, 0])

    for ref, length, which in ((inv_j, nj, 1), (inv_i, ni, 0)):
        ref[...] = inverse_entries(
            jnp.full((1, 1), coeff[0, which], F32),
            length,
            iota((length, 1), 0).astype(F32),
            iota((1, length), 1).astype(F32),
        )

    got[me] = packed[:, pl.ds(pl.multiple_of(me * 128, 128), 128)]
    for d in range(1, nc):
        fringe(d).wait_recv()
    for g in range(nc):
        vals[:, g * 128 : (g + 1) * 128] = got[g]
    cell = jnp.concatenate([cells[g : g + 1, :] for g in range(nc)], axis=1)
    hot_i = jnp.where(iota((ni, slots), 0) == cell % ni, 1.0, 0.0).astype(BF16)
    hit = iota((nj, slots), 0) == cell // ni
    dims = (((1,), (1,)), ((), ()))
    live = jnp.where(hit, vals[NV : NV + 1, :], 0.0).astype(BF16)
    filled = lax.dot_general(live, hot_i, dims, preferred_element_type=F32) > 0.5
    for v in range(NV):
        for k, part in enumerate(parts(vals[v : v + 1, :])):
            lhs[k * nj : (k + 1) * nj, :] = jnp.where(hit, part.astype(F32), 0.0).astype(BF16)
        put = lax.dot_general(lhs[...], hot_i, dims, preferred_element_type=F32)
        put = put[:nj] + put[nj : 2 * nj] + put[2 * nj :]
        full[v, :PAD] = jnp.zeros((PAD, ni), F32)
        full[v, PAD + nj :] = jnp.zeros((PAD, ni), F32)
        full[v, PAD : PAD + nj] = jnp.where(filled, put, state[v])

    def quarter_copy(v, d):
        to = (y + d) % NY
        return pltpu.make_async_remote_copy(
            src_ref=full.at[v, pl.ds(pl.multiple_of(to * quarter, 8), tall), :],
            dst_ref=slab.at[2 + y, v],
            send_sem=ya_send.at[v, d],
            recv_sem=ya_recv.at[v, d],
            device_id=at(me, z, to),
            device_id_type=MESH,
        )

    def halo_copy(v, side):
        return pltpu.make_async_remote_copy(
            src_ref=slab.at[pl.ds(4 - 2 * side, 2), v, pl.ds(PAD, quarter), :],
            dst_ref=slab.at[pl.ds(6 * side, 2), v, pl.ds(PAD, quarter), :],
            send_sem=zh_send.at[v, side],
            recv_sem=zh_recv.at[v, side],
            device_id=at(me, (high, low)[side], y),
            device_id_type=MESH,
        )

    for v in range(NV):
        for d in range(1, NY):
            quarter_copy(v, d).start()
    for v in range(NV):
        slab[2 + y, v] = full[v, pl.ds(pl.multiple_of(y * quarter, 8), tall), :]

    @pl.when(z == 0)
    def _():
        slab[0:2] = jnp.zeros((2, NV, tall, ni), F32)

    @pl.when(z == nz - 1)
    def _():
        slab[6:8] = jnp.zeros((2, NV, tall, ni), F32)

    for v in range(NV):
        for d in range(1, NY):
            quarter_copy(v, d).wait_recv()

        @pl.when(z < nz - 1)
        def _():
            halo_copy(v, 0).start()

        @pl.when(z > 0)
        def _():
            halo_copy(v, 1).start()

    for which in range(2):
        for d in range(1, NY):
            local_copy(which, d).wait_recv()
    for v in range(NV):

        @pl.when(z > 0)
        def _():
            halo_copy(v, 0).wait_recv()

        @pl.when(z < nz - 1)
        def _():
            halo_copy(v, 1).wait_recv()

    lane = iota((ROWS, ni), 1)
    for rb in range(blocks):
        top = PAD + rb * ROWS

        def layer(l, carry):
            def load(dl, dj):
                return [slab[2 + l + dl, v, top + dj : top + dj + ROWS, :] for v in range(NV)]

            here = load(0, 0)

            def shifted(by):
                keep = (lane + by >= 0) & (lane + by < ni)
                return [jnp.where(keep, pltpu.roll(f, (-by) % ni, 1), 0.0) for f in here]

            convect, near, far = None, None, None
            for direction, look in (
                (1, shifted),
                (2, lambda by: load(0, by)),
                (3, lambda by: load(by, 0)),
            ):
                ahead, behind = look(1), look(-1)
                diff = [a - b for a, b in zip(flux(ahead, direction), flux(behind, direction))]
                one = [a + b for a, b in zip(ahead, behind)]
                two = [a + b for a, b in zip(look(2), look(-2))]
                convect = diff if convect is None else [a + b for a, b in zip(convect, diff)]
                near = one if near is None else [a + b for a, b in zip(near, one)]
                far = two if far is None else [a + b for a, b in zip(far, two)]
            dt = local[0, l, rb * ROWS : (rb + 1) * ROWS, :]
            spread = 0.0625 * local[1, l, rb * ROWS : (rb + 1) * ROWS, :]
            for v in range(NV):
                smooth = far[v] - 4.0 * near[v] + 18.0 * here[v]
                done[l, rb * NV + v] = dt * (-0.5 * convect[v] - spread * smooth)
            return carry

        lax.fori_loop(0, NY, layer, 0)

        def block(v, carry):
            t = rb * NV + v
            rhs = [done[l, t] for l in range(NY)]
            for q in range(NY):
                own[q, t] = (
                    coef[q * 4] * rhs[0]
                    + coef[q * 4 + 1] * rhs[1]
                    + coef[q * 4 + 2] * rhs[2]
                    + coef[q * 4 + 3] * rhs[3]
                )
            return carry

        lax.fori_loop(0, NV, block, 0)

    @pl.when(z == 0)
    def _():
        lin[...] = jnp.zeros_like(lin)

    @pl.when(z == nz - 1)
    def _():
        rin[...] = jnp.zeros_like(rin)

    def pass_on(t, side):
        return pltpu.make_async_remote_copy(
            src_ref=(lout, rout)[side].at[t],
            dst_ref=(lin, rin)[side].at[t],
            send_sem=sc_send.at[side, t],
            recv_sem=sc_recv.at[side, t],
            device_id=at(me, (high, low)[side], y),
            device_id_type=MESH,
        )

    def home(t, q):
        return pltpu.make_async_remote_copy(
            src_ref=done.at[q, t],
            dst_ref=back.at[t % NV, pl.ds(pl.multiple_of(y * quarter + t // NV * ROWS, ROWS), ROWS), :],
            send_sem=yb_send.at[t, q],
            recv_sem=yb_recv.at[t, y],
            device_id=at(me, z, q),
            device_id_type=MESH,
        )

    def home_from(t, s):
        return pltpu.make_async_remote_copy(
            src_ref=done.at[s, t],
            dst_ref=back.at[t % NV, pl.ds(pl.multiple_of(s * quarter + t // NV * ROWS, ROWS), ROWS), :],
            send_sem=yb_send.at[t, s],
            recv_sem=yb_recv.at[t, s],
            device_id=at(me, z, s),
            device_id_type=MESH,
        )

    def scan_step(t, side):
        starts, ends = (z > 0, z < nz - 1) if side == 0 else (z < nz - 1, z > 0)
        came, gone = ((lin, lout), (rin, rout))[side]

        @pl.when(starts)
        def _():
            pass_on(t, side).wait_recv()

        @pl.when(ends)
        def _():
            first, second = came[t, 0], came[t, 1]
            for m in range(2):
                q = 2 + m if side == 0 else m
                at_q = 16 + side * 8 + q * 2
                gone[t, m] = own[q, t] + coef[at_q] * first + coef[at_q + 1] * second
            pass_on(t, side).start()

    def finish(t):
        l0, l1, r0, r1 = lin[t, 0], lin[t, 1], rin[t, 0], rin[t, 1]
        for q in range(NY):
            total = (
                own[q, t]
                + (coef[16 + q * 2] * l0 + coef[17 + q * 2] * l1)
                + (coef[24 + q * 2] * r0 + coef[25 + q * 2] * r1)
            )
            done[q, t] = total

            @pl.when(y == q)
            def _():
                back[t % NV, pl.ds(pl.multiple_of(y * quarter + t // NV * ROWS, ROWS), ROWS), :] = total

            @pl.when(y != q)
            def _():
                home(t, q).start()

    lag = jnp.clip(3 * (nz - 1 - 2 * z), -chunks, chunks)
    l_from, r_from = jnp.maximum(-lag, 0), jnp.maximum(lag, 0)
    last = jnp.maximum(l_from, r_from)

    def tick(s, carry):
        for t, job in (
            (s - l_from, lambda t: scan_step(t, 0)),
            (s - r_from, lambda t: scan_step(t, 1)),
            (s - last, finish),
        ):

            @pl.when((t >= 0) & (t < chunks))
            def _():
                job(t)

        return carry

    lax.fori_loop(0, 2 * chunks, tick, 0)

    def solve(v, carry):
        for rb in range(blocks):
            for s in range(NY):

                @pl.when(y != s)
                def _():
                    home_from(rb * NV + v, s).wait_recv()

        half = jnp.dot(
            inv_j[...], back[v], preferred_element_type=F32, precision=lax.Precision.HIGHEST
        )
        out[v] = jnp.dot(
            half, inv_i[...], preferred_element_type=F32, precision=lax.Precision.HIGHEST
        )
        return carry

    lax.fori_loop(0, NV, solve, 0)

    for d in range(1, nc):
        fringe(d).wait_send()
    for d in range(1, NY):
        for which in range(2):
            local_copy(which, d).wait_send()
        for v in range(NV):
            quarter_copy(v, d).wait_send()
    for v in range(NV):

        @pl.when(z < nz - 1)
        def _():
            halo_copy(v, 0).wait_send()

        @pl.when(z > 0)
        def _():
            halo_copy(v, 1).wait_send()

    def drain(t, carry):
        @pl.when(z < nz - 1)
        def _():
            pass_on(t, 0).wait_send()

        @pl.when(z > 0)
        def _():
            pass_on(t, 1).wait_send()

        for q in range(NY):

            @pl.when(y != q)
            def _():
                home(t, q).wait_send()

        return carry

    lax.fori_loop(0, chunks, drain, 0)


def vmem():
    return pl.BlockSpec(memory_space=pltpu.VMEM)


def body(nc, nz, state, time_step, radius, coeff, donor_cells, donor_weights, donor_group, recv_cells):
    _, nv, _, nj, ni = state.shape
    slots = recv_cells.shape[2] * recv_cells.shape[3]
    don = donor_cells.shape[3]
    quarter = nj // NY
    chunks = quarter // ROWS * NV
    field = state.reshape(nv, nj, ni)
    packed = pl.pallas_call(
        donor_kernel,
        out_shape=jax.ShapeDtypeStruct((8, slots), F32),
        in_specs=[vmem()] * 4,
        out_specs=vmem(),
        scratch_shapes=[pltpu.VMEM((nv * nj, 3 * ni), BF16), pltpu.VMEM((nv, 8, don), F32)],
        compiler_params=pltpu.CompilerParams(vmem_limit_bytes=40 * 2**20),
        name="donors",
    )(
        field,
        donor_cells.reshape(donor_cells.shape[2:]),
        donor_weights.reshape(donor_weights.shape[2:]),
        donor_group.reshape(don, 1),
    )
    dma = pltpu.SemaphoreType.DMA
    delta = pl.pallas_call(
        functools.partial(step_kernel, nc, nz),
        out_shape=jax.ShapeDtypeStruct((nv, nj, ni), F32),
        in_specs=[vmem()] * 3 + [pl.BlockSpec(memory_space=pltpu.SMEM)] + [vmem()] * 2,
        out_specs=vmem(),
        scratch_shapes=[
            pltpu.VMEM((nc, 8, 128), F32),
            pltpu.VMEM((8, slots), F32),
            pltpu.VMEM((nv, nj + 2 * PAD, ni), F32),
            pltpu.VMEM((2 * NY, nv, quarter + 2 * PAD, ni), F32),
            pltpu.VMEM((2, NY, quarter, ni), F32),
            pltpu.VMEM((NY, chunks, ROWS, ni), F32),
            pltpu.VMEM((chunks, 2, ROWS, ni), F32),
            pltpu.VMEM((chunks, 2, ROWS, ni), F32),
            pltpu.VMEM((chunks, 2, ROWS, ni), F32),
            pltpu.VMEM((chunks, 2, ROWS, ni), F32),
            pltpu.VMEM((NY, chunks, ROWS, ni), F32),
            pltpu.VMEM((nv, nj, ni), F32),
            pltpu.VMEM((nj, nj), F32),
            pltpu.VMEM((ni, ni), F32),
            pltpu.VMEM((3 * nj, slots), BF16),
            pltpu.SMEM((32,), F32),
            dma((nc,)), dma((nc,)),
            dma((2, NY)), dma((2, NY)),
            dma((nv, NY)), dma((nv, NY)),
            dma((nv, 2)), dma((nv, 2)),
            dma((2, chunks)), dma((2, chunks)),
            dma((chunks, NY)), dma((chunks, NY)),
        ],
        compiler_params=pltpu.CompilerParams(
            collective_id=0, has_side_effects=True, vmem_limit_bytes=48 * 2**20
        ),
        name="step",
    )(
        field,
        time_step.reshape(nj, ni),
        radius.reshape(nj, ni),
        coeff,
        packed,
        recv_cells.reshape(recv_cells.shape[2:]),
    )
    return delta.reshape(state.shape)


def solution(mesh):
    slabs = P("comp", "panel", None, None)
    whole = P("comp", None, "panel", None, None)
    return jax.shard_map(
        functools.partial(body, mesh.shape["comp"], mesh.shape["panel"] // NY),
        mesh=mesh,
        in_specs=(whole, slabs, slabs, P("comp", None), slabs, slabs, slabs, slabs),
        out_specs=whole,
        check_vma=False,
    )
```

time: 538 us -> 125 us (0.23)
  the two profiles are of different devices: /device:TPU:24 before, /device:TPU:2 now
where the time goes in v1:
time: 125 us
  Pallas kernels  121 us (97%)
  local copies, waits for them, and re-layouts  3.58 us (3%)
    pallas_call x1, Pallas kernels, body(): pl.pallas_call(functools.partial(step_kernel, nc, nz), out_shape=jax.Shap...  111 us
    pallas_call x1, Pallas kernels, body(): pl.pallas_call(donor_kernel, out_shape=jax.ShapeDtypeStruct((8, slots), F...  10.8 us
    unnamed x19, local copies, waits for them, and re-layouts  3.44 us

profile of v1, /device:TPU:2, one launch (start us, length us, event | category | flops | bytes accessed | tf_op | source)
XLA Modules:
  0.0 125.0 jit_solution(8456749369603027692)
XLA Ops:
  0.0 0.0 copy-start.8
  0.0 0.7 copy-done.8
  0.7 0.0 copy-start.4
  0.7 0.0 copy-start.5
  0.7 0.0 copy-start.3
  0.7 0.1 copy.10.group
  0.8 0.6 copy-done.4
  1.4 0.0 copy-done.5
  1.4 0.0 copy-start
  1.4 1.2 copy-done
  2.6 0.0 copy-start.1
  2.6 0.0 copy-start.2
  2.6 0.0 copy-start.6
  2.6 0.0 copy-start.7
  2.6 10.8 %donors.1.packed = f32[8,1024]{1,0:T(8,128)S(1)} custom-call(f32[5,192,256]{2,1,0:T(8,128)S(1)} %bitcast.10, s32[8,512]{1,0:T(8,128)S(1)} %bitcast.15, f32[8,512]{1,0:T(8,128)S(1)} %bitcast.16, s32[512,1]{1,0:T(8,128)S(1)} %copy.10.group), custom_call_target="tpu_custom_call" | custom-call | tf_op jit(solution)/shard_map/donors/pallas_call | solution.py:503
  13.5 0.0 copy-done.3
  13.5 0.0 copy-done.1
  13.5 0.0 copy-done.2
  13.5 0.0 copy-done.6
  13.5 0.0 copy-done.7
  13.5 110.5 %step.1 = f32[5,192,256]{2,1,0:T(8,128)S(1)} custom-call(f32[5,192,256]{2,1,0:T(8,128)S(1)} %bitcast.11, f32[192,256]{1,0:T(8,128)S(1)} %bitcast.13, f32[192,256]{1,0:T(8,128)S(1)} %bitcast.14, f32[1,3]{1,0:T(1,128)S(1)} %copy-done.7, f32[8,1024]{1,0:T(8,128)S(1)} %donors.1.packed, s32[8,128]{1,0:T(8,128)S(1)} %bitcast.17), custom_call_target="tpu_custom_call" | custom-call | tf_op jit(solution)/shard_map/step/pallas_call | solution.py:518
  124.0 0.9 copy.13
Async XLA Ops:
  0.0 0.7 copy-start.8
  0.7 0.7 copy-start.4
  0.7 0.7 copy-start.5
  0.7 12.8 %copy-start.3 = (f32[1,1,192,256]{3,2,1,0:T(8,128)S(1)}, f32[1,1,192,256]{3,2,1,0:T(8,128)}, u32[]{:S(2)}) copy-start(f32[1,1,192,256]{3,2,1,0:T(8,128)} %param.10) | copy-start | bytes 589828
  1.4 1.2 copy-start
  2.6 10.8 %copy-start.1 = (f32[1,5,1,192,256]{4,3,2,1,0:T(8,128)S(1)}, f32[1,5,1,192,256]{4,3,2,1,0:T(8,128)}, u32[]{:S(2)}) copy-start(f32[1,5,1,192,256]{4,3,2,1,0:T(8,128)} %param.8) | copy-start | bytes 2949124
  2.6 10.8 %copy-start.2 = (f32[1,1,192,256]{3,2,1,0:T(8,128)S(1)}, f32[1,1,192,256]{3,2,1,0:T(8,128)}, u32[]{:S(2)}) copy-start(f32[1,1,192,256]{3,2,1,0:T(8,128)} %param.9) | copy-start | bytes 589828
  2.6 10.9 %copy-start.6 = (s32[1,1,8,128]{3,2,1,0:T(8,128)S(1)}, s32[1,1,8,128]{3,2,1,0:T(8,128)}, u32[]{:S(2)}) copy-start(s32[1,1,8,128]{3,2,1,0:T(8,128)} %param.15) | copy-start | bytes 12292
  2.6 10.9 %copy-start.7 = (f32[1,3]{1,0:T(1,128)S(1)}, f32[1,3]{1,0:T(1,128)}, u32[]{:S(2)}) copy-start(f32[1,3]{1,0:T(1,128)} %coeff.1) | copy-start | bytes 40

commit v2 on v1

--- a/solution.py
+++ b/solution.py
@@ -12,6 +12,7 @@
 NV = 5
 NY = 4
 PAD = 8
+LAG = 6
 ROWS = 16
 
 
@@ -60,7 +61,7 @@
     return lax.broadcasted_iota(jnp.int32, shape, axis)
 
 
-def donor_kernel(state, cells, weights, group, packed, left, acc):
+def donors(state, cells, weights, group, packed, left, acc):
     nv, nj, ni = state.shape
     n_c, don = cells.shape
     count = packed.shape[1] // 128
@@ -121,16 +122,16 @@
 
 
 def step_kernel(
-    nc, nz, state, step_size, radius, coeff, packed, cells, out,
-    got, vals, full, slab, local, own, lin, lout, rin, rout, done, back, inv_j, inv_i, lhs, coef,
-    fx_send, fx_recv, tr_send, tr_recv, ya_send, ya_recv, zh_send, zh_recv, sc_send, sc_recv, yb_send, yb_recv,
+    nc, nz, state, step_size, radius, coeff, d_cells, d_weights, d_group, cells, out,
+    packed, left, acc, got, packets, places, full, slab, fringed, local, own, lin, lout, rin, rout, done, back, inv_j, inv_i, lhs, coef,
+    fx_send, fx_recv, pk_send, pk_recv, pl_send, pl_recv, tr_send, tr_recv, ya_send, ya_recv, zh_send, zh_recv, sc_send, sc_recv, yb_send, yb_recv,
 ):
     _, nj, ni = state.shape
     quarter = nj // NY
     tall = quarter + 2 * PAD
     blocks = quarter // ROWS
     chunks = blocks * NV
-    slots = vals.shape[1]
+    slots = packed.shape[1]
     me = lax.axis_index("comp")
     panel = lax.axis_index("panel")
     z, y = panel // NY, panel % NY
@@ -144,9 +145,42 @@
         pl.semaphore_signal(barrier, inc=1, device_id=at((me + d) % nc, z, y), device_id_type=MESH)
     for d in range(1, NY):
         pl.semaphore_signal(barrier, inc=1, device_id=at(me, z, (y + d) % NY), device_id_type=MESH)
-    pl.semaphore_signal(barrier, inc=1, device_id=at(me, low, y), device_id_type=MESH)
-    pl.semaphore_signal(barrier, inc=1, device_id=at(me, high, y), device_id_type=MESH)
-    pl.semaphore_wait(barrier, nc - 1 + NY - 1 + 2)
+    for q in range(NY):
+        pl.semaphore_signal(barrier, inc=1, device_id=at(me, low, q), device_id_type=MESH)
+        pl.semaphore_signal(barrier, inc=1, device_id=at(me, high, q), device_id_type=MESH)
+    pl.semaphore_wait(barrier, nc - 1 + NY - 1 + 2 * NY)
+
+    def quarter_copy(v, d):
+        to = (y + d) % NY
+        return pltpu.make_async_remote_copy(
+            src_ref=full.at[v, pl.ds(pl.multiple_of(to * quarter, 8), tall), :],
+            dst_ref=slab.at[2 + y, v],
+            send_sem=ya_send.at[v, d],
+            recv_sem=ya_recv.at[v, d],
+            device_id=at(me, z, to),
+            device_id_type=MESH,
+        )
+
+    def halo_copy(v, side):
+        return pltpu.make_async_remote_copy(
+            src_ref=slab.at[pl.ds(4 - 2 * side, 2), v, pl.ds(PAD, quarter), :],
+            dst_ref=slab.at[pl.ds(6 * side, 2), v, pl.ds(PAD, quarter), :],
+            send_sem=zh_send.at[v, side],
+            recv_sem=zh_recv.at[v, side],
+            device_id=at(me, (high, low)[side], y),
+            device_id_type=MESH,
+        )
+
+    def local_copy(which, d):
+        to = (y + d) % NY
+        return pltpu.make_async_remote_copy(
+            src_ref=(step_size, radius)[which].at[pl.ds(pl.multiple_of(to * quarter, 8), quarter), :],
+            dst_ref=local.at[which, y],
+            send_sem=tr_send.at[which, d],
+            recv_sem=tr_recv.at[which, d],
+            device_id=at(me, z, to),
+            device_id_type=MESH,
+        )
 
     def fringe(d):
         peer = (me + d) % nc
@@ -159,23 +193,62 @@
             device_id_type=MESH,
         )
 
-    for d in range(1, nc):
-        fringe(d).start()
-
-    def local_copy(which, d):
-        to = (y + d) % NY
+    has_low, has_high = z > 0, z < nz - 1
+    up = y >= NY - 2
+    beyond, beyond_at = jnp.where(up, high, low), (y + 6) % 8
+    reaches = (up & has_high) | (jnp.logical_not(up) & has_low)
+
+    def share(what, n):
+        ref, send, recv = ((places, pl_send, pl_recv), (packets, pk_send, pk_recv))[what]
+        slot = 2 + y if n < NY else beyond_at
         return pltpu.make_async_remote_copy(
-            src_ref=(step_size, radius)[which].at[pl.ds(pl.multiple_of(to * quarter, 8), quarter), :],
-            dst_ref=local.at[which, y],
-            send_sem=tr_send.at[which, d],
-            recv_sem=tr_recv.at[which, d],
-            device_id=at(me, z, to),
-            device_id_type=MESH,
-        )
-
-    for which in range(2):
+            src_ref=ref.at[2 + y],
+            dst_ref=ref.at[slot],
+            send_sem=send.at[n],
+            recv_sem=recv.at[slot],
+            device_id=at(me, z, (y + n) % NY) if n < NY else at(me, beyond, n - NY),
+            device_id_type=MESH,
+        )
+
+    def share_start(what):
+        for n in range(1, NY):
+            share(what, n).start()
+
+        @pl.when(reaches)
+        def _():
+            for n in range(NY, 2 * NY):
+                share(what, n).start()
+
+    def share_sent(what):
+        for n in range(1, NY):
+            share(what, n).wait_send()
+
+        @pl.when(reaches)
+        def _():
+            for n in range(NY, 2 * NY):
+                share(what, n).wait_send()
+
+    def share_came(what, slot):
+        ref, send, recv = ((places, pl_send, pl_recv), (packets, pk_send, pk_recv))[what]
+        pltpu.make_async_remote_copy(
+            src_ref=ref.at[slot],
+            dst_ref=ref.at[slot],
+            send_sem=send.at[0],
+            recv_sem=recv.at[slot],
+            device_id=at(me, z, (y + 1) % NY),
+            device_id_type=MESH,
+        ).wait_recv()
+
+    for v in range(NV):
+        full[v, :PAD] = jnp.zeros((PAD, ni), F32)
+        full[v, PAD + nj :] = jnp.zeros((PAD, ni), F32)
+        full[v, PAD : PAD + nj] = state[v]
         for d in range(1, NY):
-            local_copy(which, d).start()
+            quarter_copy(v, d).start()
+    places[2 + y] = cells[...]
+    share_start(0)
+    for v in range(NV):
+        slab[2 + y, v] = full[v, pl.ds(pl.multiple_of(y * quarter, 8), tall), :]
     mine = pl.ds(pl.multiple_of(y * quarter, 8), quarter)
     local[0, y] = step_size[mine, :]
     local[1, y] = radius[mine, :]
@@ -212,85 +285,81 @@
             iota((1, length), 1).astype(F32),
         )
 
+    donors(state, d_cells, d_weights, d_group, packed, left, acc)
+    for d in range(1, nc):
+        fringe(d).start()
     got[me] = packed[:, pl.ds(pl.multiple_of(me * 128, 128), 128)]
-    for d in range(1, nc):
-        fringe(d).wait_recv()
-    for g in range(nc):
-        vals[:, g * 128 : (g + 1) * 128] = got[g]
-    cell = jnp.concatenate([cells[g : g + 1, :] for g in range(nc)], axis=1)
-    hot_i = jnp.where(iota((ni, slots), 0) == cell % ni, 1.0, 0.0).astype(BF16)
-    hit = iota((nj, slots), 0) == cell // ni
-    dims = (((1,), (1,)), ((), ()))
-    live = jnp.where(hit, vals[NV : NV + 1, :], 0.0).astype(BF16)
-    filled = lax.dot_general(live, hot_i, dims, preferred_element_type=F32) > 0.5
-    for v in range(NV):
-        for k, part in enumerate(parts(vals[v : v + 1, :])):
-            lhs[k * nj : (k + 1) * nj, :] = jnp.where(hit, part.astype(F32), 0.0).astype(BF16)
-        put = lax.dot_general(lhs[...], hot_i, dims, preferred_element_type=F32)
-        put = put[:nj] + put[nj : 2 * nj] + put[2 * nj :]
-        full[v, :PAD] = jnp.zeros((PAD, ni), F32)
-        full[v, PAD + nj :] = jnp.zeros((PAD, ni), F32)
-        full[v, PAD : PAD + nj] = jnp.where(filled, put, state[v])
-
-    def quarter_copy(v, d):
-        to = (y + d) % NY
-        return pltpu.make_async_remote_copy(
-            src_ref=full.at[v, pl.ds(pl.multiple_of(to * quarter, 8), tall), :],
-            dst_ref=slab.at[2 + y, v],
-            send_sem=ya_send.at[v, d],
-            recv_sem=ya_recv.at[v, d],
-            device_id=at(me, z, to),
-            device_id_type=MESH,
-        )
-
-    def halo_copy(v, side):
-        return pltpu.make_async_remote_copy(
-            src_ref=slab.at[pl.ds(4 - 2 * side, 2), v, pl.ds(PAD, quarter), :],
-            dst_ref=slab.at[pl.ds(6 * side, 2), v, pl.ds(PAD, quarter), :],
-            send_sem=zh_send.at[v, side],
-            recv_sem=zh_recv.at[v, side],
-            device_id=at(me, (high, low)[side], y),
-            device_id_type=MESH,
-        )
-
-    for v in range(NV):
-        for d in range(1, NY):
-            quarter_copy(v, d).start()
-    for v in range(NV):
-        slab[2 + y, v] = full[v, pl.ds(pl.multiple_of(y * quarter, 8), tall), :]
-
-    @pl.when(z == 0)
-    def _():
-        slab[0:2] = jnp.zeros((2, NV, tall, ni), F32)
-
-    @pl.when(z == nz - 1)
-    def _():
-        slab[6:8] = jnp.zeros((2, NV, tall, ni), F32)
-
     for v in range(NV):
         for d in range(1, NY):
             quarter_copy(v, d).wait_recv()
 
-        @pl.when(z < nz - 1)
+        @pl.when(has_high)
         def _():
             halo_copy(v, 0).start()
 
-        @pl.when(z > 0)
+        @pl.when(has_low)
         def _():
             halo_copy(v, 1).start()
 
+    for d in range(1, nc):
+        fringe(d).wait_recv()
+    packets[2 + y] = jnp.concatenate([got[g] for g in range(nc)], axis=1)
+    share_start(1)
+    for which in range(2):
+        for d in range(1, NY):
+            local_copy(which, d).start()
+
+    dims = (((1,), (1,)), ((), ()))
+
+    def place(n, carry):
+        l = (n + 2) % 8
+        here = ((l >= 2) | has_low) & ((l < 6) | has_high)
+
+        @pl.when(here & (l != 2 + y))
+        def _():
+            share_came(0, l)
+            share_came(1, l)
+
+        for side, first in ((0, 0), (1, 6)):
+
+            @pl.when(here & (l == first))
+            def _():
+                for v in range(NV):
+                    halo_copy(v, side).wait_recv()
+
+        @pl.when(jnp.logical_not(here))
+        def _():
+            fringed[l] = jnp.zeros((NV, tall, ni), F32)
+
+        @pl.when(here)
+        def _():
+            where, values = places[l], packets[l]
+            cell = jnp.concatenate([where[g : g + 1, :] for g in range(nc)], axis=1)
+            row = cell // ni - (y * quarter - PAD)
+            hot_i = jnp.where(iota((ni, slots), 0) == cell % ni, 1.0, 0.0).astype(BF16)
+            hot_j = jnp.where(iota((tall, slots), 0) == row, 1.0, 0.0).astype(BF16)
+            split = [part.astype(F32) for part in parts(values)]
+
+            def rows_of(line):
+                sixteen = jnp.broadcast_to(line, (16, slots)).astype(BF16)
+                return hot_j * jnp.concatenate([sixteen] * (tall // 16), axis=0)
+
+            for v in range(NV):
+                for k in range(3):
+                    lhs[(3 * v + k) * tall : (3 * v + k + 1) * tall, :] = rows_of(split[k][v : v + 1])
+            lhs[3 * NV * tall :, :] = rows_of(values[NV : NV + 1])
+            put = lax.dot_general(lhs[...], hot_i, dims, preferred_element_type=F32)
+            filled = put[3 * NV * tall :] > 0.5
+            for v in range(NV):
+                hi, mid, lo = (put[(3 * v + k) * tall : (3 * v + k + 1) * tall] for k in range(3))
+                fringed[l, v] = jnp.where(filled, hi + mid + lo, slab[l, v])
+
+        return carry
+
+    lax.fori_loop(0, 8, place, 0)
     for which in range(2):
         for d in range(1, NY):
             local_copy(which, d).wait_recv()
-    for v in range(NV):
-
-        @pl.when(z > 0)
-        def _():
-            halo_copy(v, 0).wait_recv()
-
-        @pl.when(z < nz - 1)
-        def _():
-            halo_copy(v, 1).wait_recv()
 
     lane = iota((ROWS, ni), 1)
     for rb in range(blocks):
@@ -298,7 +367,7 @@
 
         def layer(l, carry):
             def load(dl, dj):
-                return [slab[2 + l + dl, v, top + dj : top + dj + ROWS, :] for v in range(NV)]
+                return [fringed[2 + l + dl, v, top + dj : top + dj + ROWS, :] for v in range(NV)]
 
             here = load(0, 0)
 
@@ -321,9 +390,18 @@
                 far = two if far is None else [a + b for a, b in zip(far, two)]
             dt = local[0, l, rb * ROWS : (rb + 1) * ROWS, :]
             spread = 0.0625 * local[1, l, rb * ROWS : (rb + 1) * ROWS, :]
+            rhs = []
             for v in range(NV):
                 smooth = far[v] - 4.0 * near[v] + 18.0 * here[v]
-                done[l, rb * NV + v] = dt * (-0.5 * convect[v] - spread * smooth)
+                rhs.append(dt * (-0.5 * convect[v] - spread * smooth))
+            rhs = jnp.dot(
+                jnp.concatenate(rhs, axis=0),
+                inv_i[...],
+                preferred_element_type=F32,
+                precision=lax.Precision.HIGHEST,
+            )
+            for v in range(NV):
+                done[l, rb * NV + v] = rhs[v * ROWS : (v + 1) * ROWS]
             return carry
 
         lax.fori_loop(0, NY, layer, 0)
@@ -360,23 +438,14 @@
             device_id_type=MESH,
         )
 
-    def home(t, q):
+    def home(rb, q, source):
+        run = pl.ds(rb * NV, NV)
         return pltpu.make_async_remote_copy(
-            src_ref=done.at[q, t],
-            dst_ref=back.at[t % NV, pl.ds(pl.multiple_of(y * quarter + t // NV * ROWS, ROWS), ROWS), :],
-            send_sem=yb_send.at[t, q],
-            recv_sem=yb_recv.at[t, y],
+            src_ref=done.at[q, run],
+            dst_ref=back.at[source, run],
+            send_sem=yb_send.at[rb, q],
+            recv_sem=yb_recv.at[rb, source],
             device_id=at(me, z, q),
-            device_id_type=MESH,
-        )
-
-    def home_from(t, s):
-        return pltpu.make_async_remote_copy(
-            src_ref=done.at[s, t],
-            dst_ref=back.at[t % NV, pl.ds(pl.multiple_of(s * quarter + t // NV * ROWS, ROWS), ROWS), :],
-            send_sem=yb_send.at[t, s],
-            recv_sem=yb_recv.at[t, s],
-            device_id=at(me, z, s),
             device_id_type=MESH,
         )
 
@@ -397,61 +466,70 @@
                 gone[t, m] = own[q, t] + coef[at_q] * first + coef[at_q + 1] * second
             pass_on(t, side).start()
 
-    def finish(t):
-        l0, l1, r0, r1 = lin[t, 0], lin[t, 1], rin[t, 0], rin[t, 1]
+    def finish(rb):
+        def one(v, carry):
+            t = rb * NV + v
+            l0, l1, r0, r1 = lin[t, 0], lin[t, 1], rin[t, 0], rin[t, 1]
+            for q in range(NY):
+                done[q, t] = (
+                    own[q, t]
+                    + (coef[16 + q * 2] * l0 + coef[17 + q * 2] * l1)
+                    + (coef[24 + q * 2] * r0 + coef[25 + q * 2] * r1)
+                )
+            return carry
+
+        lax.fori_loop(0, NV, one, 0)
         for q in range(NY):
-            total = (
-                own[q, t]
-                + (coef[16 + q * 2] * l0 + coef[17 + q * 2] * l1)
-                + (coef[24 + q * 2] * r0 + coef[25 + q * 2] * r1)
-            )
-            done[q, t] = total
 
             @pl.when(y == q)
             def _():
-                back[t % NV, pl.ds(pl.multiple_of(y * quarter + t // NV * ROWS, ROWS), ROWS), :] = total
+                back[q, rb * NV : (rb + 1) * NV] = done[q, rb * NV : (rb + 1) * NV]
 
             @pl.when(y != q)
             def _():
-                home(t, q).start()
-
-    lag = jnp.clip(3 * (nz - 1 - 2 * z), -chunks, chunks)
+                home(rb, q, y).start()
+
+    lag = jnp.clip(LAG * (nz - 1 - 2 * z), -chunks, chunks)
     l_from, r_from = jnp.maximum(-lag, 0), jnp.maximum(lag, 0)
     last = jnp.maximum(l_from, r_from)
 
     def tick(s, carry):
-        for t, job in (
-            (s - l_from, lambda t: scan_step(t, 0)),
-            (s - r_from, lambda t: scan_step(t, 1)),
-            (s - last, finish),
-        ):
+        for side, t in enumerate((s - l_from, s - r_from)):
 
             @pl.when((t >= 0) & (t < chunks))
             def _():
-                job(t)
+                scan_step(t, side)
+
+        for rb in range(blocks):
+
+            @pl.when(s == last + (rb + 1) * NV - 1)
+            def _():
+                finish(rb)
 
         return carry
 
-    lax.fori_loop(0, 2 * chunks, tick, 0)
+    lax.fori_loop(0, last + chunks, tick, 0)
+
+    for rb in range(blocks):
+        for s in range(NY):
+
+            @pl.when(y != s)
+            def _():
+                home(rb, s, s).wait_recv()
 
     def solve(v, carry):
-        for rb in range(blocks):
-            for s in range(NY):
-
-                @pl.when(y != s)
-                def _():
-                    home_from(rb * NV + v, s).wait_recv()
-
-        half = jnp.dot(
-            inv_j[...], back[v], preferred_element_type=F32, precision=lax.Precision.HIGHEST
+        plane = jnp.concatenate(
+            [back[s, rb * NV + v] for s in range(NY) for rb in range(blocks)], axis=0
         )
         out[v] = jnp.dot(
-            half, inv_i[...], preferred_element_type=F32, precision=lax.Precision.HIGHEST
+            inv_j[...], plane, preferred_element_type=F32, precision=lax.Precision.HIGHEST
         )
         return carry
 
     lax.fori_loop(0, NV, solve, 0)
 
+    share_sent(0)
+    share_sent(1)
     for d in range(1, nc):
         fringe(d).wait_send()
     for d in range(1, NY):
@@ -478,15 +556,15 @@
         def _():
             pass_on(t, 1).wait_send()
 
+        return carry
+
+    lax.fori_loop(0, chunks, drain, 0)
+    for rb in range(blocks):
         for q in range(NY):
 
             @pl.when(y != q)
             def _():
-                home(t, q).wait_send()
-
-        return carry
-
-    lax.fori_loop(0, chunks, drain, 0)
+                home(rb, q, y).wait_send()
 
 
 def vmem():
@@ -500,30 +578,21 @@
     quarter = nj // NY
     chunks = quarter // ROWS * NV
     field = state.reshape(nv, nj, ni)
-    packed = pl.pallas_call(
-        donor_kernel,
-        out_shape=jax.ShapeDtypeStruct((8, slots), F32),
-        in_specs=[vmem()] * 4,
-        out_specs=vmem(),
-        scratch_shapes=[pltpu.VMEM((nv * nj, 3 * ni), BF16), pltpu.VMEM((nv, 8, don), F32)],
-        compiler_params=pltpu.CompilerParams(vmem_limit_bytes=40 * 2**20),
-        name="donors",
-    )(
-        field,
-        donor_cells.reshape(donor_cells.shape[2:]),
-        donor_weights.reshape(donor_weights.shape[2:]),
-        donor_group.reshape(don, 1),
-    )
     dma = pltpu.SemaphoreType.DMA
     delta = pl.pallas_call(
         functools.partial(step_kernel, nc, nz),
         out_shape=jax.ShapeDtypeStruct((nv, nj, ni), F32),
-        in_specs=[vmem()] * 3 + [pl.BlockSpec(memory_space=pltpu.SMEM)] + [vmem()] * 2,
+        in_specs=[vmem()] * 3 + [pl.BlockSpec(memory_space=pltpu.SMEM)] + [vmem()] * 4,
         out_specs=vmem(),
         scratch_shapes=[
+            pltpu.VMEM((8, slots), F32),
+            pltpu.VMEM((nv * nj, 3 * ni), BF16),
+            pltpu.VMEM((nv, 8, don), F32),
             pltpu.VMEM((nc, 8, 128), F32),
-            pltpu.VMEM((8, slots), F32),
+            pltpu.VMEM((2 * NY, 8, slots), F32),
+            pltpu.VMEM((2 * NY,) + recv_cells.shape[2:], jnp.int32),
             pltpu.VMEM((nv, nj + 2 * PAD, ni), F32),
+            pltpu.VMEM((2 * NY, nv, quarter + 2 * PAD, ni), F32),
             pltpu.VMEM((2 * NY, nv, quarter + 2 * PAD, ni), F32),
             pltpu.VMEM((2, NY, quarter, ni), F32),
             pltpu.VMEM((NY, chunks, ROWS, ni), F32),
@@ -532,17 +601,19 @@
             pltpu.VMEM((chunks, 2, ROWS, ni), F32),
             pltpu.VMEM((chunks, 2, ROWS, ni), F32),
             pltpu.VMEM((NY, chunks, ROWS, ni), F32),
-            pltpu.VMEM((nv, nj, ni), F32),
+            pltpu.VMEM((NY, chunks, ROWS, ni), F32),
             pltpu.VMEM((nj, nj), F32),
             pltpu.VMEM((ni, ni), F32),
-            pltpu.VMEM((3 * nj, slots), BF16),
+            pltpu.VMEM(((3 * nv + 1) * (quarter + 2 * PAD), slots), BF16),
             pltpu.SMEM((32,), F32),
             dma((nc,)), dma((nc,)),
+            dma((2 * NY,)), dma((2 * NY,)),
+            dma((2 * NY,)), dma((2 * NY,)),
             dma((2, NY)), dma((2, NY)),
             dma((nv, NY)), dma((nv, NY)),
             dma((nv, 2)), dma((nv, 2)),
             dma((2, chunks)), dma((2, chunks)),
-            dma((chunks, NY)), dma((chunks, NY)),
+            dma((quarter // ROWS, NY)), dma((quarter // ROWS, NY)),
         ],
         compiler_params=pltpu.CompilerParams(
             collective_id=0, has_side_effects=True, vmem_limit_bytes=48 * 2**20
@@ -553,7 +624,9 @@
         time_step.reshape(nj, ni),
         radius.reshape(nj, ni),
         coeff,
-        packed,
+        donor_cells.reshape(donor_cells.shape[2:]),
+        donor_weights.reshape(donor_weights.shape[2:]),
+        donor_group.reshape(don, 1),
         recv_cells.reshape(recv_cells.shape[2:]),
     )
     return delta.reshape(state.shape)

time: 125 us -> 117 us (0.936)
  Pallas kernels: 121 us -> 113 us
    pallas_call x1 -> x0, Pallas kernels: 10.8 us -> none  [body(): pl.pallas_call(donor_kernel, out_shape=jax.ShapeDtypeStruct((8, slots), F...]
    pallas_call x1, Pallas kernels: 111 us -> 113 us  [body(): pl.pallas_call(functools.partial(step_kernel, nc, nz), out_shape=jax.Shap...]
    unnamed x19 -> x15, local copies, waits for them, and re-layouts: 3.44 us -> 3.13 us
where the time goes in v2:
time: 117 us
  Pallas kernels  113 us (97%)
  local copies, waits for them, and re-layouts  3.99 us (3%)
    pallas_call x1, Pallas kernels, body(): pl.pallas_call(functools.partial(step_kernel, nc, nz), out_shape=jax.Shap...  113 us
    unnamed x15, local copies, waits for them, and re-layouts  3.13 us

profile of v2, /device:TPU:2, one launch (start us, length us, event | category | flops | bytes accessed | tf_op | source)
XLA Modules:
  0.0 116.7 jit_solution(12682818813721283126)
XLA Ops:
  0.0 0.0 copy-start.1
  0.0 0.0 copy-start.3
  0.0 0.0 copy-start.4
  0.0 0.0 copy-start.5
  0.0 0.0 copy-start.6
  0.0 0.9 copy.10.d_group
  0.9 0.0 copy-done.1
  0.9 0.0 copy-done.3
  0.9 0.0 copy-done.4
  0.9 0.0 copy-done.5
  1.0 0.0 copy-done.6
  1.0 0.0 copy-start
  1.0 1.2 %copy-done = f32[1,5,1,192,256]{4,3,2,1,0:T(8,128)S(1)} copy-done((f32[1,5,1,192,256]{4,3,2,1,0:T(8,128)S(1)}, f32[1,5,1,192,256]{4,3,2,1,0:T(8,128)}, u32[]{:S(2)}) %copy-start) | copy-done | bytes 983064
  2.2 0.0 copy-start.2
  2.2 0.9 copy-done.2
  3.1 112.7 %step.1 = f32[5,192,256]{2,1,0:T(8,128)S(1)} custom-call(f32[5,192,256]{2,1,0:T(8,128)S(1)} %bitcast.11, f32[192,256]{1,0:T(8,128)S(1)} %bitcast.12, f32[192,256]{1,0:T(8,128)S(1)} %bitcast.13, f32[1,3]{1,0:T(1,128)S(1)} %copy-done.6, s32[8,512]{1,0:T(8,128)S(1)} %bitcast.14, f32[8,512]{1,0:T(8,128)S(1)} %bitcast.15, s32[512,1]{1,0:T(8,128)S(1)} %copy.10.d_group, ...), custom_call_target="tpu_custom_call" | custom-call | tf_op jit(solution)/shard_map/step/pallas_call | solution.py:582
  115.8 0.9 copy.13
Async XLA Ops:
  0.0 0.9 copy-start.1
  0.0 0.9 copy-start.3
  0.0 0.9 copy-start.4
  0.0 0.9 copy-start.5
  0.0 0.9 copy-start.6
  1.0 1.2 %copy-start = (f32[1,5,1,192,256]{4,3,2,1,0:T(8,128)S(1)}, f32[1,5,1,192,256]{4,3,2,1,0:T(8,128)}, u32[]{:S(2)}) copy-start(f32[1,5,1,192,256]{4,3,2,1,0:T(8,128)} %param.8) | copy-start | bytes 2949124
  2.2 0.9 copy-start.2

commit v3 on v2

--- a/solution.py
+++ b/solution.py
@@ -18,9 +18,15 @@
 
 def parts(x):
     hi = x.astype(BF16)
-    rest = x - hi.astype(F32)
-    mid = rest.astype(BF16)
-    return hi, mid, (rest - mid.astype(F32)).astype(BF16)
+    return hi, (x - hi.astype(F32)).astype(BF16)
+
+
+def product(a, b):
+    return (
+        jnp.dot(a[0], b[0], preferred_element_type=F32)
+        + jnp.dot(a[0], b[1], preferred_element_type=F32)
+        + jnp.dot(a[1], b[0], preferred_element_type=F32)
+    )
 
 
 def inverse_entries(h, length, i, j):
@@ -79,7 +85,7 @@
             weight = weights[pl.ds(c, 1), span]
             col = jnp.where(iota((ni, width), 0) == cell % ni, 1.0, 0.0).astype(BF16)
             got = jnp.dot(
-                left[...], jnp.concatenate([col, col, col], axis=0), preferred_element_type=F32
+                left[...], jnp.concatenate([col, col], axis=0), preferred_element_type=F32
             )
             row = jnp.where(iota((nj, width), 0) == cell // ni, weight, 0.0)
             for v in range(nv):
@@ -94,17 +100,15 @@
         values + [jnp.ones((1, don), F32), jnp.zeros((8 - nv - 1, don), F32)], axis=0
     )
     mine = group[...]
-    hot = jnp.where(iota((don, 128), 1) == mine, 1.0, 0.0)
-    before = jnp.where(iota((don, don), 1) < iota((don, don), 0), 1.0, 0.0).astype(BF16)
-    ahead = jnp.dot(before, hot.astype(BF16), preferred_element_type=F32)
-    slot = jnp.sum(hot * ahead, axis=1, keepdims=True).astype(jnp.int32)
-    target = mine * 128 + slot
-    place = jnp.where(iota((don, count * 128), 1) == target, 1.0, 0.0).astype(BF16)
-    hi, mid, lo = parts(values)
-    packed[...] = (
-        jnp.dot(hi, place, preferred_element_type=F32)
-        + jnp.dot(mid, place, preferred_element_type=F32)
-        + jnp.dot(lo, place, preferred_element_type=F32)
+    hot = jnp.where(iota((16, don), 0) == mine, 1.0, 0.0)
+    before = jnp.where(iota((don, don), 0) < iota((don, don), 1), 1.0, 0.0).astype(BF16)
+    ahead = jnp.dot(hot.astype(BF16), before, preferred_element_type=F32)
+    target = mine * 128 + jnp.sum(hot * ahead, axis=0, keepdims=True).astype(jnp.int32)
+    place = jnp.where(iota((count * 128, don), 0) == target, 1.0, 0.0).astype(BF16)
+    dims = (((1,), (1,)), ((), ()))
+    hi, lo = parts(values)
+    packed[...] = lax.dot_general(hi, place, dims, preferred_element_type=F32) + lax.dot_general(
+        lo, place, dims, preferred_element_type=F32
     )
 
 
@@ -247,6 +251,9 @@
             quarter_copy(v, d).start()
     places[2 + y] = cells[...]
     share_start(0)
+    for which in range(2):
+        for d in range(1, NY):
+            local_copy(which, d).start()
     for v in range(NV):
         slab[2 + y, v] = full[v, pl.ds(pl.multiple_of(y * quarter, 8), tall), :]
     mine = pl.ds(pl.multiple_of(y * quarter, 8), quarter)
@@ -278,11 +285,13 @@
             coef[16 + side * 8 + q * 2 + 1] = jnp.where(edge, 0.0, ((t * a - s * b) * det)[0, 0])
 
     for ref, length, which in ((inv_j, nj, 1), (inv_i, ni, 0)):
-        ref[...] = inverse_entries(
-            jnp.full((1, 1), coeff[0, which], F32),
-            length,
-            iota((length, 1), 0).astype(F32),
-            iota((1, length), 1).astype(F32),
+        ref[0], ref[1] = parts(
+            inverse_entries(
+                jnp.full((1, 1), coeff[0, which], F32),
+                length,
+                iota((length, 1), 0).astype(F32),
+                iota((1, length), 1).astype(F32),
+            )
         )
 
     donors(state, d_cells, d_weights, d_group, packed, left, acc)
@@ -305,9 +314,6 @@
         fringe(d).wait_recv()
     packets[2 + y] = jnp.concatenate([got[g] for g in range(nc)], axis=1)
     share_start(1)
-    for which in range(2):
-        for d in range(1, NY):
-            local_copy(which, d).start()
 
     dims = (((1,), (1,)), ((), ()))
 
@@ -345,14 +351,14 @@
                 return hot_j * jnp.concatenate([sixteen] * (tall // 16), axis=0)
 
             for v in range(NV):
-                for k in range(3):
-                    lhs[(3 * v + k) * tall : (3 * v + k + 1) * tall, :] = rows_of(split[k][v : v + 1])
-            lhs[3 * NV * tall :, :] = rows_of(values[NV : NV + 1])
+                for k in range(2):
+                    lhs[(2 * v + k) * tall : (2 * v + k + 1) * tall, :] = rows_of(split[k][v : v + 1])
+            lhs[2 * NV * tall :, :] = rows_of(values[NV : NV + 1])
             put = lax.dot_general(lhs[...], hot_i, dims, preferred_element_type=F32)
-            filled = put[3 * NV * tall :] > 0.5
+            filled = put[2 * NV * tall :] > 0.5
             for v in range(NV):
-                hi, mid, lo = (put[(3 * v + k) * tall : (3 * v + k + 1) * tall] for k in range(3))
-                fringed[l, v] = jnp.where(filled, hi + mid + lo, slab[l, v])
+                hi, lo = (put[(2 * v + k) * tall : (2 * v + k + 1) * tall] for k in range(2))
+                fringed[l, v] = jnp.where(filled, hi + lo, slab[l, v])
 
         return carry
 
@@ -360,6 +366,24 @@
     for which in range(2):
         for d in range(1, NY):
             local_copy(which, d).wait_recv()
+
+    def pass_on(t, side):
+        return pltpu.make_async_remote_copy(
+            src_ref=(lout, rout)[side].at[t],
+            dst_ref=(lin, rin)[side].at[t],
+            send_sem=sc_send.at[side, t],
+            recv_sem=sc_recv.at[side, t],
+            device_id=at(me, (high, low)[side], y),
+            device_id_type=MESH,
+        )
+
+    @pl.when(z == 0)
+    def _():
+        lin[...] = jnp.zeros_like(lin)
+
+    @pl.when(z == nz - 1)
+    def _():
+        rin[...] = jnp.zeros_like(rin)
 
     lane = iota((ROWS, ni), 1)
     for rb in range(blocks):
@@ -394,49 +418,35 @@
             for v in range(NV):
                 smooth = far[v] - 4.0 * near[v] + 18.0 * here[v]
                 rhs.append(dt * (-0.5 * convect[v] - spread * smooth))
-            rhs = jnp.dot(
-                jnp.concatenate(rhs, axis=0),
-                inv_i[...],
-                preferred_element_type=F32,
-                precision=lax.Precision.HIGHEST,
-            )
             for v in range(NV):
-                done[l, rb * NV + v] = rhs[v * ROWS : (v + 1) * ROWS]
+                done[l, rb * NV + v] = rhs[v]
             return carry
 
         lax.fori_loop(0, NY, layer, 0)
 
-        def block(v, carry):
-            t = rb * NV + v
-            rhs = [done[l, t] for l in range(NY)]
+        run = slice(rb * NV, (rb + 1) * NV)
+        solved = product(parts(done[:, run].reshape(NY * NV * ROWS, ni)), inv_i)
+        solved = solved.reshape(NY, NV, ROWS, ni)
+        for v in range(NV):
             for q in range(NY):
-                own[q, t] = (
-                    coef[q * 4] * rhs[0]
-                    + coef[q * 4 + 1] * rhs[1]
-                    + coef[q * 4 + 2] * rhs[2]
-                    + coef[q * 4 + 3] * rhs[3]
+                own[q, rb * NV + v] = (
+                    coef[q * 4] * solved[0, v]
+                    + coef[q * 4 + 1] * solved[1, v]
+                    + coef[q * 4 + 2] * solved[2, v]
+                    + coef[q * 4 + 3] * solved[3, v]
                 )
-            return carry
-
-        lax.fori_loop(0, NV, block, 0)
-
-    @pl.when(z == 0)
-    def _():
-        lin[...] = jnp.zeros_like(lin)
-
-    @pl.when(z == nz - 1)
-    def _():
-        rin[...] = jnp.zeros_like(rin)
-
-    def pass_on(t, side):
-        return pltpu.make_async_remote_copy(
-            src_ref=(lout, rout)[side].at[t],
-            dst_ref=(lin, rin)[side].at[t],
-            send_sem=sc_send.at[side, t],
-            recv_sem=sc_recv.at[side, t],
-            device_id=at(me, (high, low)[side], y),
-            device_id_type=MESH,
-        )
+
+        @pl.when(z == 0)
+        def _():
+            for t in range(rb * NV, (rb + 1) * NV):
+                lout[t] = own[2:4, t]
+                pass_on(t, 0).start()
+
+        @pl.when(z == nz - 1)
+        def _():
+            for t in range(rb * NV, (rb + 1) * NV):
+                rout[t] = own[0:2, t]
+                pass_on(t, 1).start()
 
     def home(rb, q, source):
         run = pl.ds(rb * NV, NV)
@@ -450,25 +460,24 @@
         )
 
     def scan_step(t, side):
-        starts, ends = (z > 0, z < nz - 1) if side == 0 else (z < nz - 1, z > 0)
+        edge, other = (z == 0, z == nz - 1) if side == 0 else (z == nz - 1, z == 0)
         came, gone = ((lin, lout), (rin, rout))[side]
 
-        @pl.when(starts)
+        @pl.when(jnp.logical_not(edge))
         def _():
             pass_on(t, side).wait_recv()
 
-        @pl.when(ends)
-        def _():
-            first, second = came[t, 0], came[t, 1]
-            for m in range(2):
-                q = 2 + m if side == 0 else m
-                at_q = 16 + side * 8 + q * 2
-                gone[t, m] = own[q, t] + coef[at_q] * first + coef[at_q + 1] * second
-            pass_on(t, side).start()
+            @pl.when(jnp.logical_not(other))
+            def _():
+                first, second = came[t, 0], came[t, 1]
+                for m in range(2):
+                    q = 2 + m if side == 0 else m
+                    at_q = 16 + side * 8 + q * 2
+                    gone[t, m] = own[q, t] + coef[at_q] * first + coef[at_q + 1] * second
+                pass_on(t, side).start()
 
     def finish(rb):
-        def one(v, carry):
-            t = rb * NV + v
+        for t in range(rb * NV, (rb + 1) * NV):
             l0, l1, r0, r1 = lin[t, 0], lin[t, 1], rin[t, 0], rin[t, 1]
             for q in range(NY):
                 done[q, t] = (
@@ -476,9 +485,6 @@
                     + (coef[16 + q * 2] * l0 + coef[17 + q * 2] * l1)
                     + (coef[24 + q * 2] * r0 + coef[25 + q * 2] * r1)
                 )
-            return carry
-
-        lax.fori_loop(0, NV, one, 0)
         for q in range(NY):
 
             @pl.when(y == q)
@@ -489,26 +495,27 @@
             def _():
                 home(rb, q, y).start()
 
-    lag = jnp.clip(LAG * (nz - 1 - 2 * z), -chunks, chunks)
-    l_from, r_from = jnp.maximum(-lag, 0), jnp.maximum(lag, 0)
-    last = jnp.maximum(l_from, r_from)
-
-    def tick(s, carry):
-        for side, t in enumerate((s - l_from, s - r_from)):
-
-            @pl.when((t >= 0) & (t < chunks))
-            def _():
-                scan_step(t, side)
-
-        for rb in range(blocks):
-
-            @pl.when(s == last + (rb + 1) * NV - 1)
-            def _():
-                finish(rb)
-
-        return carry
-
-    lax.fori_loop(0, last + chunks, tick, 0)
+    def run_scan(side, lag):
+        for s in range(lag + chunks):
+            if s < chunks:
+                scan_step(s, side)
+            if s >= lag:
+                scan_step(s - lag, 1 - side)
+                if (s - lag + 1) % NV == 0:
+                    finish((s - lag) // NV)
+
+    middle = nz // 2
+    near = min(LAG, chunks)
+    for here, side, lag in (
+        (z < middle - 1, 0, chunks),
+        (z == middle - 1, 0, near),
+        (z == middle, 1, near),
+        (z > middle, 1, chunks),
+    ):
+
+        @pl.when(here)
+        def _():
+            run_scan(side, lag)
 
     for rb in range(blocks):
         for s in range(NY):
@@ -521,9 +528,7 @@
         plane = jnp.concatenate(
             [back[s, rb * NV + v] for s in range(NY) for rb in range(blocks)], axis=0
         )
-        out[v] = jnp.dot(
-            inv_j[...], plane, preferred_element_type=F32, precision=lax.Precision.HIGHEST
-        )
+        out[v] = product(inv_j, parts(plane))
         return carry
 
     lax.fori_loop(0, NV, solve, 0)
@@ -586,7 +591,7 @@
         out_specs=vmem(),
         scratch_shapes=[
             pltpu.VMEM((8, slots), F32),
-            pltpu.VMEM((nv * nj, 3 * ni), BF16),
+            pltpu.VMEM((nv * nj, 2 * ni), BF16),
             pltpu.VMEM((nv, 8, don), F32),
             pltpu.VMEM((nc, 8, 128), F32),
             pltpu.VMEM((2 * NY, 8, slots), F32),
@@ -602,9 +607,9 @@
             pltpu.VMEM((chunks, 2, ROWS, ni), F32),
             pltpu.VMEM((NY, chunks, ROWS, ni), F32),
             pltpu.VMEM((NY, chunks, ROWS, ni), F32),
-            pltpu.VMEM((nj, nj), F32),
-            pltpu.VMEM((ni, ni), F32),
-            pltpu.VMEM(((3 * nv + 1) * (quarter + 2 * PAD), slots), BF16),
+            pltpu.VMEM((2, nj, nj), BF16),
+            pltpu.VMEM((2, ni, ni), BF16),
+            pltpu.VMEM(((2 * nv + 1) * (quarter + 2 * PAD), slots), BF16),
             pltpu.SMEM((32,), F32),
             dma((nc,)), dma((nc,)),
             dma((2 * NY,)), dma((2 * NY,)),
@@ -626,7 +631,7 @@
         coeff,
         donor_cells.reshape(donor_cells.shape[2:]),
         donor_weights.reshape(donor_weights.shape[2:]),
-        donor_group.reshape(don, 1),
+        donor_group.reshape(1, don),
         recv_cells.reshape(recv_cells.shape[2:]),
     )
     return delta.reshape(state.shape)

time: 117 us -> 112 us (0.957)
  Pallas kernels: 113 us -> 105 us
  local copies, waits for them, and re-layouts: 3.99 us -> 6.13 us
    pallas_call x1, Pallas kernels: 113 us -> 105 us  [body(): pl.pallas_call(functools.partial(step_kernel, nc, nz), out_shape=jax.Shap...]
    unnamed x15 -> x17, local copies, waits for them, and re-layouts: 3.13 us -> 6.13 us
where the time goes in v3:
time: 112 us
  Pallas kernels  105 us (94%)
  local copies, waits for them, and re-layouts  6.13 us (5%)
    pallas_call x1, Pallas kernels, body(): pl.pallas_call(functools.partial(step_kernel, nc, nz), out_shape=jax.Shap...  105 us
    unnamed x17, local copies, waits for them, and re-layouts  6.13 us

profile of v3, /device:TPU:2, one launch (start us, length us, event | category | flops | bytes accessed | tf_op | source)
XLA Modules:
  0.0 111.5 jit_solution(6382968147437695319)
XLA Ops:
  0.0 0.0 copy-start.5
  0.0 0.0 copy-start.6
  0.0 0.0 copy-start.7
  0.0 0.7 copy-done.5
  0.7 0.0 copy-done.6
  0.7 0.0 copy-done.7
  0.7 0.0 copy-start
  0.7 1.2 %copy-done = f32[1,5,1,192,256]{4,3,2,1,0:T(8,128)S(1)} copy-done((f32[1,5,1,192,256]{4,3,2,1,0:T(8,128)S(1)}, f32[1,5,1,192,256]{4,3,2,1,0:T(8,128)}, u32[]{:S(2)}) %copy-start) | copy-done | bytes 983064
  1.9 0.0 copy-start.1
  1.9 0.9 copy-done.1
  2.8 0.0 copy-start.2
  2.8 0.9 copy-done.2
  3.8 0.0 copy-start.3
  3.8 0.7 copy-done.3
  4.5 0.0 copy-start.4
  4.5 0.7 copy-done.4
  5.2 105.4 %step.1 = f32[5,192,256]{2,1,0:T(8,128)S(1)} custom-call(f32[5,192,256]{2,1,0:T(8,128)S(1)} %bitcast.11, f32[192,256]{1,0:T(8,128)S(1)} %bitcast.12, f32[192,256]{1,0:T(8,128)S(1)} %bitcast.13, f32[1,3]{1,0:T(1,128)S(1)} %copy-done.7, s32[8,512]{1,0:T(8,128)S(1)} %bitcast.14, f32[8,512]{1,0:T(8,128)S(1)} %bitcast.15, s32[1,512]{1,0:T(1,128)S(1)} %bitcast.17, ...), custom_call_target="tpu_custom_call" | custom-call | tf_op jit(solution)/shard_map/step/pallas_call | solution.py:587
  110.6 0.9 copy.11
Async XLA Ops:
  0.0 0.7 copy-start.5
  0.0 0.7 copy-start.6
  0.0 0.7 copy-start.7
  0.7 1.2 %copy-start = (f32[1,5,1,192,256]{4,3,2,1,0:T(8,128)S(1)}, f32[1,5,1,192,256]{4,3,2,1,0:T(8,128)}, u32[]{:S(2)}) copy-start(f32[1,5,1,192,256]{4,3,2,1,0:T(8,128)} %param.8) | copy-start | bytes 2949124
  1.9 0.9 copy-start.1
  2.8 0.9 copy-start.2
  3.8 0.7 copy-start.3
  4.5 0.7 copy-start.4

commit v4 on v3

--- a/solution.py
+++ b/solution.py
@@ -67,7 +67,7 @@
     return lax.broadcasted_iota(jnp.int32, shape, axis)
 
 
-def donors(state, cells, weights, group, packed, left, acc):
+def donors(state, cells, weights, group, packed, left, acc, between):
     nv, nj, ni = state.shape
     n_c, don = cells.shape
     count = packed.shape[1] // 128
@@ -93,7 +93,9 @@
                 acc[v, :, span] += jnp.sum(term.reshape(nj // 8, 8, width), axis=0)
             return carry
 
-        lax.fori_loop(0, n_c, one, 0)
+        for half in range(2):
+            lax.fori_loop(half * n_c // 2, (half + 1) * n_c // 2, one, 0)
+            between()
 
     values = [jnp.sum(acc[v], axis=0, keepdims=True) for v in range(nv)]
     values = jnp.concatenate(
@@ -251,9 +253,6 @@
             quarter_copy(v, d).start()
     places[2 + y] = cells[...]
     share_start(0)
-    for which in range(2):
-        for d in range(1, NY):
-            local_copy(which, d).start()
     for v in range(NV):
         slab[2 + y, v] = full[v, pl.ds(pl.multiple_of(y * quarter, 8), tall), :]
     mine = pl.ds(pl.multiple_of(y * quarter, 8), quarter)
@@ -294,26 +293,39 @@
             )
         )
 
-    donors(state, d_cells, d_weights, d_group, packed, left, acc)
+    turn = iter(range(-1, NV))
+
+    def halos(v):
+        for d in range(1, NY):
+            quarter_copy(v, d).wait_recv()
+
+        @pl.when(has_high)
+        def _():
+            halo_copy(v, 0).start()
+
+        @pl.when(has_low)
+        def _():
+            halo_copy(v, 1).start()
+
+    def between():
+        v = next(turn)
+        if v >= 0:
+            halos(v)
+
+    donors(state, d_cells, d_weights, d_group, packed, left, acc, between)
     for d in range(1, nc):
         fringe(d).start()
     got[me] = packed[:, pl.ds(pl.multiple_of(me * 128, 128), 128)]
-    for v in range(NV):
-        for d in range(1, NY):
-            quarter_copy(v, d).wait_recv()
-
-        @pl.when(has_high)
-        def _():
-            halo_copy(v, 0).start()
-
-        @pl.when(has_low)
-        def _():
-            halo_copy(v, 1).start()
+    for v in turn:
+        halos(v)
 
     for d in range(1, nc):
         fringe(d).wait_recv()
     packets[2 + y] = jnp.concatenate([got[g] for g in range(nc)], axis=1)
     share_start(1)
+    for which in range(2):
+        for d in range(1, NY):
+            local_copy(which, d).start()
 
     dims = (((1,), (1,)), ((), ()))
 

time: 112 us -> 110 us (0.982)
  Pallas kernels: 105 us -> 103 us
    pallas_call x1, Pallas kernels: 105 us -> 103 us  [body(): pl.pallas_call(functools.partial(step_kernel, nc, nz), out_shape=jax.Shap...]
where the time goes in v4:
time: 110 us; the launch traced here: 109 us
  Pallas kernels  103 us (94%)
  local copies, waits for them, and re-layouts  6.13 us (6%)
    pallas_call x1, Pallas kernels, body(): pl.pallas_call(functools.partial(step_kernel, nc, nz), out_shape=jax.Shap...  103 us
    unnamed x17, local copies, waits for them, and re-layouts  6.13 us

profile of v4, /device:TPU:2, one launch (start us, length us, event | category | flops | bytes accessed | tf_op | source)
XLA Modules:
  0.0 109.3 jit_solution(8599592744570463373)
XLA Ops:
  0.0 0.0 copy-start.5
  0.0 0.0 copy-start.6
  0.0 0.0 copy-start.7
  0.0 0.7 copy-done.5
  0.7 0.0 copy-done.6
  0.7 0.0 copy-done.7
  0.7 0.0 copy-start
  0.7 1.2 %copy-done = f32[1,5,1,192,256]{4,3,2,1,0:T(8,128)S(1)} copy-done((f32[1,5,1,192,256]{4,3,2,1,0:T(8,128)S(1)}, f32[1,5,1,192,256]{4,3,2,1,0:T(8,128)}, u32[]{:S(2)}) %copy-start) | copy-done | bytes 983064
  1.9 0.0 copy-start.1
  1.9 0.9 copy-done.1
  2.8 0.0 copy-start.2
  2.8 0.9 copy-done.2
  3.8 0.0 copy-start.3
  3.8 0.7 copy-done.3
  4.5 0.0 copy-start.4
  4.5 0.7 copy-done.4
  5.2 103.1 %step.1 = f32[5,192,256]{2,1,0:T(8,128)S(1)} custom-call(f32[5,192,256]{2,1,0:T(8,128)S(1)} %bitcast.11, f32[192,256]{1,0:T(8,128)S(1)} %bitcast.12, f32[192,256]{1,0:T(8,128)S(1)} %bitcast.13, f32[1,3]{1,0:T(1,128)S(1)} %copy-done.7, s32[8,512]{1,0:T(8,128)S(1)} %bitcast.14, f32[8,512]{1,0:T(8,128)S(1)} %bitcast.15, s32[1,512]{1,0:T(1,128)S(1)} %bitcast.17, ...), custom_call_target="tpu_custom_call" | custom-call | tf_op jit(solution)/shard_map/step/pallas_call | solution.py:599
  108.3 0.9 copy.11
Async XLA Ops:
  0.0 0.7 copy-start.5
  0.0 0.7 copy-start.6
  0.0 0.7 copy-start.7
  0.7 1.2 %copy-start = (f32[1,5,1,192,256]{4,3,2,1,0:T(8,128)S(1)}, f32[1,5,1,192,256]{4,3,2,1,0:T(8,128)}, u32[]{:S(2)}) copy-start(f32[1,5,1,192,256]{4,3,2,1,0:T(8,128)} %param.8) | copy-start | bytes 2949124
  1.9 0.9 copy-start.1
  2.8 0.9 copy-start.2
  3.8 0.7 copy-start.3
  4.5 0.7 copy-start.4

commit v5 on v4

--- a/solution.py
+++ b/solution.py
@@ -12,8 +12,8 @@
 NV = 5
 NY = 4
 PAD = 8
-LAG = 6
-ROWS = 16
+LAG = 12
+ROWS = 8
 
 
 def parts(x):

time: 110 us -> 108 us (0.982)
  Pallas kernels: 103 us -> 101 us
    pallas_call x1, Pallas kernels: 103 us -> 101 us  [body(): pl.pallas_call(functools.partial(step_kernel, nc, nz), out_shape=jax.Shap...]
where the time goes in v5:
time: 108 us; the launch traced here: 107 us
  Pallas kernels  101 us (94%)
  local copies, waits for them, and re-layouts  6.13 us (6%)
    pallas_call x1, Pallas kernels, body(): pl.pallas_call(functools.partial(step_kernel, nc, nz), out_shape=jax.Shap...  101 us
    unnamed x17, local copies, waits for them, and re-layouts  6.13 us

profile of v5, /device:TPU:2, one launch (start us, length us, event | category | flops | bytes accessed | tf_op | source)
XLA Modules:
  0.0 107.3 jit_solution(6766703002347557954)
XLA Ops:
  0.0 0.0 copy-start.5
  0.0 0.0 copy-start.6
  0.0 0.0 copy-start.7
  0.0 0.7 copy-done.5
  0.7 0.0 copy-done.6
  0.7 0.0 copy-done.7
  0.7 0.0 copy-start
  0.7 1.2 %copy-done = f32[1,5,1,192,256]{4,3,2,1,0:T(8,128)S(1)} copy-done((f32[1,5,1,192,256]{4,3,2,1,0:T(8,128)S(1)}, f32[1,5,1,192,256]{4,3,2,1,0:T(8,128)}, u32[]{:S(2)}) %copy-start) | copy-done | bytes 983064
  1.9 0.0 copy-start.1
  1.9 0.9 copy-done.1
  2.8 0.0 copy-start.2
  2.8 0.9 copy-done.2
  3.8 0.0 copy-start.3
  3.8 0.7 copy-done.3
  4.5 0.0 copy-start.4
  4.5 0.7 copy-done.4
  5.2 101.1 %step.1 = f32[5,192,256]{2,1,0:T(8,128)S(1)} custom-call(f32[5,192,256]{2,1,0:T(8,128)S(1)} %bitcast.11, f32[192,256]{1,0:T(8,128)S(1)} %bitcast.12, f32[192,256]{1,0:T(8,128)S(1)} %bitcast.13, f32[1,3]{1,0:T(1,128)S(1)} %copy-done.7, s32[8,512]{1,0:T(8,128)S(1)} %bitcast.14, f32[8,512]{1,0:T(8,128)S(1)} %bitcast.15, s32[1,512]{1,0:T(1,128)S(1)} %bitcast.17, ...), custom_call_target="tpu_custom_call" | custom-call | tf_op jit(solution)/shard_map/step/pallas_call | solution.py:599
  106.3 0.9 copy.11
Async XLA Ops:
  0.0 0.7 copy-start.5
  0.0 0.7 copy-start.6
  0.0 0.7 copy-start.7
  0.7 1.2 %copy-start = (f32[1,5,1,192,256]{4,3,2,1,0:T(8,128)S(1)}, f32[1,5,1,192,256]{4,3,2,1,0:T(8,128)}, u32[]{:S(2)}) copy-start(f32[1,5,1,192,256]{4,3,2,1,0:T(8,128)} %param.8) | copy-start | bytes 2949124
  1.9 0.9 copy-start.1
  2.8 0.9 copy-start.2
  3.8 0.7 copy-start.3
  4.5 0.7 copy-start.4
